TPU v7x, 128 devices: a whole 4x4x4 slice. The times are simulated.
128 devices in a mesh: dp: 4 (over y), row: 8 (over z, core), col: 4 (over x).
Axes of the slice: x: 4, y: 4, z: 4, core: 2. Of those that a mesh axis runs over, the one named last changes fastest.
Arguments:
- gradients: bfloat16 [4, 8192, 14336], P('dp', 'row', 'col'), may hold values from -6 to 6
- test_matrix: int32 [14336, 512], P('col'), may hold values from -3 to 3
- old_basis: float32 [8192, 512], P('row'), may hold values from -0.0625 to 0.0625
- first_moment: float32 [512, 14336], P(('dp', 'row'), 'col'), may hold values from -24 to 24
- second_moment: float32 [512, 14336], P(('dp', 'row'), 'col'), may hold values from 1 to 16
Outputs:
- projected: float32 [512, 14336], P(('dp', 'row'), 'col')
- first_moment_new: float32 [512, 14336], P(('dp', 'row'), 'col')
- second_moment_new: float32 [512, 14336], P(('dp', 'row'), 'col')
All inputs are finite; a program needn't handle non-finite values.
Results may differ from a plain program's by a relative error of at most 0.0023.
Values sent between devices are 32-bit elements; how exact they have to be, the bound alone decides.
A program may use at most 128 MiB of HBM per device.

v0:
```python
import jax
import jax.numpy as jnp
from jax import lax
from jax.sharding import PartitionSpec as P

highest = lax.Precision.HIGHEST


def from_partner(value, axis, bit):
    return lax.ppermute(value, axis, [(i, i ^ 1 << bit) for i in range(lax.axis_size(axis))])


def gram_of(row_block):
    return lax.dot_general(
        row_block,
        row_block,
        (((0,), (0,)), ((), ())),
        precision=highest,
        preferred_element_type=jnp.float32,
    )


def basis_from(lower_factor, sketch_part):
    return jax.scipy.linalg.solve_triangular(lower_factor, sketch_part.T, lower=True).T


def local(gradients, test_matrix, old_basis, first_moment, second_moment):
    replica_grad = gradients[0]
    test_values = test_matrix.astype(jnp.bfloat16)
    partial_value = jnp.dot(replica_grad, test_values, preferred_element_type=jnp.float32)
    sketch = lax.psum(partial_value, ("dp", "col"))
    upper_factor = jnp.linalg.cholesky(gram_of(sketch)).T
    for bit_level in range(lax.axis_size("row").bit_length() - 1):
        partner = from_partner(upper_factor, "row", bit_level)
        upper_factor = jnp.linalg.cholesky(gram_of(upper_factor) + gram_of(partner)).T
    new_basis = basis_from(upper_factor.T, sketch)
    basis_low = new_basis.astype(jnp.bfloat16)
    local_correlation = lax.dot_general(
        new_basis,
        old_basis,
        (((0,), (0,)), ((), ())),
        precision=highest,
        preferred_element_type=jnp.float32,
    )
    correlation = lax.psum(local_correlation, "row")
    rank_dev = first_moment.shape[0]
    rank_start = lax.axis_index(("dp", "row")) * rank_dev
    projected = lax.psum_scatter(
        lax.dot_general(
            basis_low, replica_grad, (((0,), (0,)), ((), ())), preferred_element_type=jnp.float32
        ),
        ("dp", "row"),
        scatter_dimension=0,
        tiled=True,
    )
    own_rows = lax.dynamic_slice_in_dim(correlation, rank_start, rank_dev, 0)
    squared = own_rows * own_rows
    turned_first = jnp.dot(
        own_rows,
        lax.all_gather(first_moment, ("dp", "row"), axis=0, tiled=True),
        precision=highest,
        preferred_element_type=jnp.float32,
    )
    turned_second = jnp.dot(
        squared,
        lax.all_gather(second_moment, ("dp", "row"), axis=0, tiled=True),
        precision=highest,
        preferred_element_type=jnp.float32,
    )
    first_new = 0.9 * turned_first + 0.1 * projected
    second_new = 0.95 * turned_second + 0.05 * projected * projected
    return (projected, first_new, second_new)


def solution(mesh):
    in_specs = (
        P("dp", "row", "col"),
        P("col", None),
        P("row", None),
        P(("dp", "row"), "col"),
        P(("dp", "row"), "col"),
    )
    out_specs = (P(("dp", "row"), "col"), P(("dp", "row"), "col"), P(("dp", "row"), "col"))
    return jax.shard_map(local, mesh=mesh, in_specs=in_specs, out_specs=out_specs, check_vma=False)
```

profile of v0, /device:TPU:0, one launch (start us, length us, event | category | flops | bytes accessed | tf_op | source)
XLA Modules:
  0.0 833.6 jit_solution(15446949937610158620)
XLA Ops:
  8.1 10.6 %fusion.2 = f32[1024,512]{1,0:T(8,128)} fusion(bf16[1,1024,3584]{2,1,0:T(8,128)(2,1)} %param.6, s32[3584,512]{1,0:T(8,128)} %param.7), kind=kOutput, calls=%fused_computation.4 | convolution fusion | flops 3759931392 | bytes 16777216 | tf_op jit(solution)/shard_map/dot_general | solution.py:30
  18.9 93.3 %all-reduce.4.cloned.1.call-done = f32[1024,512]{1,0:T(8,128)} async-done(((f32[1024,512]{1,0:T(8,128)}), f32[1024,512]{1,0:T(8,128)}) %all-reduce.4.cloned.1.call-update) | async-done | bytes 2097168 | tf_op jit(solution)/shard_map/psum | solution.py:31
  112.2 5.7 fusion.148
  121.7 11.7 %cholesky.462 = f32[128,128]{1,0:T(8,128)S(1)} custom-call(f32[128,128]{1,0:T(8,128)S(1)} %cholesky.746), custom_call_target="Cholesky" | custom-call | tf_op jit(solution)/shard_map/jit(cholesky)/cholesky | solution.py:32
  133.4 9.8 %custom-call.34 = f32[1,128,128]{1,2,0:T(8,128)S(1)} custom-call(f32[1,128,128]{2,1,0:T(8,128)S(1)} %get-tuple-element.61), custom_call_target="InvertDiagBlocksLowerTriangular" | custom-call | tf_op jit(solution)/shard_map/jit(cholesky)/cholesky | solution.py:32
  145.9 12.1 %cholesky.481 = f32[128,128]{1,0:T(8,128)S(1)} custom-call(f32[128,128]{1,0:T(8,128)S(1)} %cholesky.750), custom_call_target="Cholesky" | custom-call | tf_op jit(solution)/shard_map/jit(cholesky)/cholesky | solution.py:32
  158.0 9.8 %custom-call.35 = f32[1,128,128]{1,2,0:T(8,128)S(1)} custom-call(f32[1,128,128]{2,1,0:T(8,128)S(1)} %get-tuple-element.58), custom_call_target="InvertDiagBlocksLowerTriangular" | custom-call | tf_op jit(solution)/shard_map/jit(cholesky)/cholesky | solution.py:32
  169.4 11.7 %cholesky.502 = f32[128,128]{1,0:T(8,128)S(1)} custom-call(f32[128,128]{1,0:T(8,128)S(1)} %cholesky.755), custom_call_target="Cholesky" | custom-call | tf_op jit(solution)/shard_map/jit(cholesky)/cholesky | solution.py:32
  181.8 9.8 %custom-call.36 = f32[1,128,128]{1,2,0:T(8,128)S(1)} custom-call(f32[1,128,128]{2,1,0:T(8,128)S(1)} %get-tuple-element.55), custom_call_target="InvertDiagBlocksLowerTriangular" | custom-call | tf_op jit(solution)/shard_map/jit(cholesky)/cholesky | solution.py:32
  193.0 11.9 %cholesky.519 = f32[128,128]{1,0:T(8,128)S(1)} custom-call(f32[128,128]{1,0:T(8,128)S(1)} %convolution_subtract_fusion.4), custom_call_target="Cholesky" | custom-call | tf_op jit(solution)/shard_map/jit(cholesky)/cholesky | solution.py:32
  217.3 11.7 %cholesky.534 = f32[128,128]{1,0:T(8,128)S(1)} custom-call(f32[128,128]{1,0:T(8,128)S(1)} %cholesky.759), custom_call_target="Cholesky" | custom-call | tf_op jit(solution)/shard_map/jit(cholesky)/cholesky | solution.py:35
  229.2 9.8 %custom-call.37 = f32[1,128,128]{1,2,0:T(8,128)S(1)} custom-call(f32[1,128,128]{2,1,0:T(8,128)S(1)} %get-tuple-element.51), custom_call_target="InvertDiagBlocksLowerTriangular" | custom-call | tf_op jit(solution)/shard_map/jit(cholesky)/cholesky | solution.py:35
  241.5 12.1 %cholesky.553 = f32[128,128]{1,0:T(8,128)S(1)} custom-call(f32[128,128]{1,0:T(8,128)S(1)} %cholesky.763), custom_call_target="Cholesky" | custom-call | tf_op jit(solution)/shard_map/jit(cholesky)/cholesky | solution.py:35
  254.9 9.8 %custom-call.38 = f32[1,128,128]{1,2,0:T(8,128)S(1)} custom-call(f32[1,128,128]{2,1,0:T(8,128)S(1)} %get-tuple-element.48), custom_call_target="InvertDiagBlocksLowerTriangular" | custom-call | tf_op jit(solution)/shard_map/jit(cholesky)/cholesky | solution.py:35
  266.3 11.7 %cholesky.574 = f32[128,128]{1,0:T(8,128)S(1)} custom-call(f32[128,128]{1,0:T(8,128)S(1)} %cholesky.768), custom_call_target="Cholesky" | custom-call | tf_op jit(solution)/shard_map/jit(cholesky)/cholesky | solution.py:35
  278.7 9.8 %custom-call.39 = f32[1,128,128]{1,2,0:T(8,128)S(1)} custom-call(f32[1,128,128]{2,1,0:T(8,128)S(1)} %get-tuple-element.45), custom_call_target="InvertDiagBlocksLowerTriangular" | custom-call | tf_op jit(solution)/shard_map/jit(cholesky)/cholesky | solution.py:35
  290.1 11.7 %cholesky.591 = f32[128,128]{1,0:T(8,128)S(1)} custom-call(f32[128,128]{1,0:T(8,128)S(1)} %slice_subtract_fusion.8), custom_call_target="Cholesky" | custom-call | tf_op jit(solution)/shard_map/jit(cholesky)/cholesky | solution.py:35
  308.8 21.7 %collective-permute-done.1 = f32[512,512]{0,1:T(8,128)S(1)} collective-permute-done((f32[512,512]{0,1:T(8,128)S(1)}, f32[512,512]{0,1:T(8,128)S(1)}, u32[]{:S(2)}, u32[]{:S(2)}) %collective-permute-start.1) | collective-permute-done | bytes 1048608 | tf_op jit(solution)/shard_map/ppermute | solution.py:10
  336.1 11.7 %cholesky.606 = f32[128,128]{1,0:T(8,128)S(1)} custom-call(f32[128,128]{1,0:T(8,128)S(1)} %cholesky.772), custom_call_target="Cholesky" | custom-call | tf_op jit(solution)/shard_map/jit(cholesky)/cholesky | solution.py:35
  348.0 9.8 %custom-call.40 = f32[1,128,128]{1,2,0:T(8,128)S(1)} custom-call(f32[1,128,128]{2,1,0:T(8,128)S(1)} %get-tuple-element.41), custom_call_target="InvertDiagBlocksLowerTriangular" | custom-call | tf_op jit(solution)/shard_map/jit(cholesky)/cholesky | solution.py:35
  360.4 12.1 %cholesky.625 = f32[128,128]{1,0:T(8,128)S(1)} custom-call(f32[128,128]{1,0:T(8,128)S(1)} %cholesky.776), custom_call_target="Cholesky" | custom-call | tf_op jit(solution)/shard_map/jit(cholesky)/cholesky | solution.py:35
  373.8 9.8 %custom-call.41 = f32[1,128,128]{1,2,0:T(8,128)S(1)} custom-call(f32[1,128,128]{2,1,0:T(8,128)S(1)} %get-tuple-element.38), custom_call_target="InvertDiagBlocksLowerTriangular" | custom-call | tf_op jit(solution)/shard_map/jit(cholesky)/cholesky | solution.py:35
  385.2 11.7 %cholesky.646 = f32[128,128]{1,0:T(8,128)S(1)} custom-call(f32[128,128]{1,0:T(8,128)S(1)} %cholesky.781), custom_call_target="Cholesky" | custom-call | tf_op jit(solution)/shard_map/jit(cholesky)/cholesky | solution.py:35
  397.6 9.8 %custom-call.42 = f32[1,128,128]{1,2,0:T(8,128)S(1)} custom-call(f32[1,128,128]{2,1,0:T(8,128)S(1)} %get-tuple-element.35), custom_call_target="InvertDiagBlocksLowerTriangular" | custom-call | tf_op jit(solution)/shard_map/jit(cholesky)/cholesky | solution.py:35
  409.0 11.7 %cholesky.663 = f32[128,128]{1,0:T(8,128)S(1)} custom-call(f32[128,128]{1,0:T(8,128)S(1)} %slice_subtract_fusion.7), custom_call_target="Cholesky" | custom-call | tf_op jit(solution)/shard_map/jit(cholesky)/cholesky | solution.py:35
  425.1 3.2 collective-permute-start.2
  430.1 21.1 %collective-permute-done.2 = f32[512,512]{0,1:T(8,128)} collective-permute-done((f32[512,512]{0,1:T(8,128)}, f32[512,512]{0,1:T(8,128)}, u32[]{:S(2)}, u32[]{:S(2)}) %collective-permute-start.2) | collective-permute-done | bytes 1048608 | tf_op jit(solution)/shard_map/ppermute | solution.py:10
  451.2 3.4 convolution_add_fusion
  458.4 11.7 %cholesky.678 = f32[128,128]{1,0:T(8,128)S(1)} custom-call(f32[128,128]{1,0:T(8,128)S(1)} %cholesky.785), custom_call_target="Cholesky" | custom-call | tf_op jit(solution)/shard_map/jit(cholesky)/cholesky | solution.py:35
  470.3 9.8 %custom-call.43 = f32[1,128,128]{1,2,0:T(8,128)S(1)} custom-call(f32[1,128,128]{2,1,0:T(8,128)S(1)} %get-tuple-element.31), custom_call_target="InvertDiagBlocksLowerTriangular" | custom-call | tf_op jit(solution)/shard_map/jit(cholesky)/cholesky | solution.py:35
  482.6 12.1 %cholesky.697 = f32[128,128]{1,0:T(8,128)S(1)} custom-call(f32[128,128]{1,0:T(8,128)S(1)} %cholesky.789), custom_call_target="Cholesky" | custom-call | tf_op jit(solution)/shard_map/jit(cholesky)/cholesky | solution.py:35
  496.0 9.8 %custom-call.44 = f32[1,128,128]{1,2,0:T(8,128)S(1)} custom-call(f32[1,128,128]{2,1,0:T(8,128)S(1)} %get-tuple-element.28), custom_call_target="InvertDiagBlocksLowerTriangular" | custom-call | tf_op jit(solution)/shard_map/jit(cholesky)/cholesky | solution.py:35
  507.4 11.7 %cholesky.718 = f32[128,128]{1,0:T(8,128)S(1)} custom-call(f32[128,128]{1,0:T(8,128)S(1)} %cholesky.794), custom_call_target="Cholesky" | custom-call | tf_op jit(solution)/shard_map/jit(cholesky)/cholesky | solution.py:35
  519.8 9.8 %custom-call.45 = f32[1,128,128]{1,2,0:T(8,128)S(1)} custom-call(f32[1,128,128]{2,1,0:T(8,128)S(1)} %get-tuple-element.25), custom_call_target="InvertDiagBlocksLowerTriangular" | custom-call | tf_op jit(solution)/shard_map/jit(cholesky)/cholesky | solution.py:35
  531.2 11.7 %cholesky.735 = f32[128,128]{1,0:T(8,128)S(1)} custom-call(f32[128,128]{1,0:T(8,128)S(1)} %slice_subtract_fusion.6), custom_call_target="Cholesky" | custom-call | tf_op jit(solution)/shard_map/jit(cholesky)/cholesky | solution.py:35
  547.2 14.0 %while.1 = (s32[]{:T(128)}, f32[512,512]{1,0:T(8,128)}, s32[4,2]{0,1:T(2,128)S(1)}, f32[4,128,128]{2,1,0:T(8,128)}, s32[]{:T(128)}) while((s32[]{:T(128)}, f32[512,512]{1,0:T(8,128)}, s32[4,2]{0,1:T(2,128)S(1)}, f32[4,128,128]{2,1,0:T(8,128)}, s32[]{:T(128)}) %tuple.53), condition=%wide.while_cond, body=%wide.while_body.sunk | while | flops 2 | bytes 132705 | solution.py:24
  547.8 2.9 bitcast_dynamic-update-slice_fusion.2
  551.3 2.9 bitcast_dynamic-update-slice_fusion.2
  554.8 2.9 bitcast_dynamic-update-slice_fusion.2
  561.1 40.1 %custom-call.24 = f32[4,128,128]{1,2,0:T(8,128)S(1)} custom-call(f32[4,128,128]{2,1,0:T(8,128)} %get-tuple-element.11), custom_call_target="InvertDiagBlocksLowerTriangular" | custom-call | tf_op jit(solution)/shard_map/jit(_solve_triangular)/triangular_solve | solution.py:24
  609.2 3.8 fusion.13
  614.5 4.5 fusion.16
  619.9 10.3 %fusion = f32[512,3584]{1,0:T(8,128)} fusion(bf16[1,1024,3584]{2,1,0:T(8,128)(2,1)} %param.6, f32[128,1024]{1,0:T(8,128)} %copy-done.7, f32[128,1024]{1,0:T(8,128)} %copy-done.2, f32[128,1024]{1,0:T(8,128)S(1)} %fusion.78, f32[128,1024]{1,0:T(8,128)S(1)} %fusion.32), kind=kOutput, calls=%fused_computation.2 | convolution fusion | flops 3762290688 | bytes 16777216 | tf_op jit(solution)/shard_map/dot_general | solution.py:49
  630.9 55.4 %all-reduce.6.cloned.1.call-done = f32[512,512]{1,0:T(8,128)} async-done(((f32[512,512]{1,0:T(8,128)}), f32[512,512]{1,0:T(8,128)}) %all-reduce.6.cloned.1.call-update) | async-done | bytes 1048592 | tf_op jit(solution)/shard_map/psum | solution.py:45
  686.2 79.9 %reduce-scatter.2.cloned.1.call-done = f32[16,3584]{1,0:T(8,128)} async-done(((f32[512,3584]{1,0:T(8,128)}), f32[16,3584]{1,0:T(8,128)}) %reduce-scatter.2.cloned.1.call-update) | async-done | bytes 229392 | tf_op jit(solution)/shard_map/reduce_scatter | solution.py:48
  766.2 7.4 fusion.4
  773.5 44.9 %all-gather.3.cloned.1.call-done = f32[512,3584]{1,0:T(8,128)} async-done(((f32[16,3584]{1,0:T(8,128)}), f32[512,3584]{1,0:T(8,128)}) %all-gather.3.cloned.1.call-update) | async-done | bytes 7340048 | tf_op jit(solution)/shard_map/all_gather | solution.py:60
  818.4 7.3 fusion.5
  (138 shorter events, 78.7 us)
Async XLA Ops:
  8.0 606.5 %copy-start = (f32[1024,512]{1,0:T(8,128)S(1)}, f32[1024,512]{1,0:T(8,128)}, u32[]{:S(2)}) copy-start(f32[1024,512]{1,0:T(8,128)} %param.8) | copy-start | bytes 6291460
  8.0 104.2 %all-reduce.4.cloned.1.call-start = ((), (), s32[]{:S(2)}) async-start(), calls=%async_computation.1 | async-start | bytes 4194304 | tf_op jit(solution)/shard_map/psum | solution.py:31
  18.6 667.6 %all-reduce.6.cloned.1.call-start = ((), (), s32[]{:S(2)}) async-start(), calls=%async_computation.3 | async-start | bytes 2097152 | tf_op jit(solution)/shard_map/psum | solution.py:45
  120.7 1.0 copy-start.6
  208.9 2.7 collective-permute-start
  216.3 1.0 copy-start.4
  305.2 25.3 %collective-permute-start.1 = (f32[512,512]{0,1:T(8,128)S(1)}, f32[512,512]{0,1:T(8,128)S(1)}, u32[]{:S(2)}, u32[]{:S(2)}) collective-permute-start(f32[512,512]{0,1:T(8,128)S(1)} %fusion.28), channel_id=1, source_target_pairs={{0,8},{4,12},{8,0},{12,4},{16,24},{20,28},{24,16},{28,20},{1,9},{5... | collective-permute-start | bytes 3145736 | tf_op jit(solution)/shard_map/ppermute | solution.py:10
  335.2 1.0 copy-start.5
  425.1 26.1 %collective-permute-start.2 = (f32[512,512]{0,1:T(8,128)}, f32[512,512]{0,1:T(8,128)}, u32[]{:S(2)}, u32[]{:S(2)}) collective-permute-start(f32[512,512]{0,1:T(8,128)} %fusion.30), channel_id=1, source_target_pairs={{0,16},{4,20},{8,24},{12,28},{16,0},{20,4},{24,8},{28,12},{1,17},{... | collective-permute-start | bytes 3145736 | tf_op jit(solution)/shard_map/ppermute | solution.py:10
  457.4 1.0 copy-start.3
  601.3 4.6 copy-start.1
  609.2 4.5 copy-start.2
  613.7 0.8 copy-start.7
  619.1 67.1 %all-gather.5.cloned.1.call-start = ((), (), s32[]{:S(2)}) async-start(), calls=%async_computation.5 | async-start | bytes 7569408 | tf_op jit(solution)/shard_map/all_gather | solution.py:66
  619.7 146.5 %reduce-scatter.2.cloned.1.call-start = ((), (), s32[]{:S(2)}) async-start(), calls=%async_computation.2 | async-start | bytes 7569408 | tf_op jit(solution)/shard_map/reduce_scatter | solution.py:48
  630.3 188.1 %all-gather.3.cloned.1.call-start = ((), (), s32[]{:S(2)}) async-start(), calls=%async_computation.4 | async-start | bytes 7569408 | tf_op jit(solution)/shard_map/all_gather | solution.py:60
  766.2 52.3 %copy-start.8 = (f32[16,3584]{1,0:T(8,128)S(1)}, f32[16,3584]{1,0:T(8,128)}, u32[]{:S(2)}) copy-start(f32[16,3584]{1,0:T(8,128)} %reduce-scatter.2.cloned.1.call-done) | copy-start | bytes 688132
Sparse Core Ops, SparseCore 0:
  18.8 93.3 all-reduce.3
  619.2 66.9 all-reduce.5
Sparse Core Ops, SparseCore 1:
  621.8 51.6 all-gather.4
  677.7 88.4 reduce-scatter.1
  768.3 50.1 all-gather.2
where the time goes:
time: 838 us; the launch traced here: 834 us
  other arithmetic  365 us (44%)
  waiting for transfers between devices  318 us (38%)
  matrix products  93.3 us (11%)
  between operations  26.7 us (3%)
  local copies, waits for them, and re-layouts  24.6 us (3%)
    another operation x45, other arithmetic, local(): jnp.linalg.cholesky(gram_of(upper_factor) + gram_of(partner))  238 us
    psum x1, waiting for transfers between devices, local(): sketch = lax.psum(partial_value, ('dp', 'col'))  93.3 us
    reduce_scatter x1, waiting for transfers between devices, local(): lax.psum_scatter(lax.dot_general(basis_low, replica_grad, (((0,), (0,)),...  79.9 us
    another operation x14, other arithmetic, local(): upper_factor = jnp.linalg.cholesky(gram_of(sketch)).T  78.9 us
    psum x1, waiting for transfers between devices, local(): correlation = lax.psum(local_correlation, 'row')  55.4 us
    all_gather x1, waiting for transfers between devices, local(): lax.all_gather(first_moment, ('dp', 'row'), axis=0, tiled=True)  44.9 us
    ppermute x3, waiting for transfers between devices, from_partner(): lax.ppermute(value, axis, [(i, i ^ 1 << bit) for i in range(lax.axis_size...  43.6 us
    another operation x3, other arithmetic, basis_from(): jax.scipy.linalg.solve_triangular(lower_factor, sketch_part.T, lower=True)  41.2 us
  transfers between devices with their start and end apart: 8, of which 7 were waited for; matrix products, arithmetic and copies ran while one was open for 3% of the time, Pallas kernels for 0%

commit v1 on v0

v1 whole, which is shorter than its diff:
```python
import functools
import jax, jax.numpy as jnp
from jax import lax
from jax.experimental import pallas as pl
from jax.experimental.pallas import tpu as pltpu
from jax.sharding import PartitionSpec as P

HI = lax.Precision.HIGHEST
f32 = jnp.float32


def factor_diag(block, group):
    size = block.shape[0]
    tiles = size // 8
    z = [block[8 * b : 8 * b + 8, :] for b in range(tiles)]
    lane = lax.broadcasted_iota(jnp.int32, (8, size), 1)
    sub = lax.broadcasted_iota(jnp.int32, (8, size), 0)
    full = lambda v: jnp.broadcast_to(v, (8, size))
    for b in range(tiles):
        pivots = jnp.ones((8, size), f32)
        for r in range(0, 8, group):
            j = 8 * b + r
            piv = [[full(z[b][r + t : r + t + 1, j + s : j + s + 1]) for s in range(group)] for t in range(group)]
            inside = (lane >= j) & (lane < j + group)
            rows = [
                jnp.where(inside, (lane == j + t).astype(f32), full(z[b][r + t : r + t + 1, :])) for t in range(group)
            ]
            inv = []
            for t in range(group):
                pivots = jnp.where(sub == r + t, piv[t][t], pivots)
                inv.append(1.0 / piv[t][t])
                for u in range(t + 1, group):
                    m = piv[t][u] * inv[t]
                    for s in range(u, group):
                        piv[u][s] = piv[u][s] - m * piv[t][s]
                    rows[u] = rows[u] - m * rows[t]
            for i in range(b, tiles):
                cols = [full_col(z[i], j + t, size) for t in range(group)]
                acc = jnp.where(inside, (sub - r == lane - j).astype(f32) if i == b else 0.0, z[i])
                for t in range(group):
                    m = cols[t] * inv[t]
                    for u in range(t + 1, group):
                        cols[u] = cols[u] - m * piv[t][u]
                    if i == b:
                        m = jnp.where(sub > r + t, m, 0.0)
                    acc = acc - m * rows[t]
                z[i] = acc
        z[b] = z[b] * lax.rsqrt(pivots)
    out = jnp.concatenate(z, axis=0)
    i = lax.broadcasted_iota(jnp.int32, (size, size), 0)
    k = lax.broadcasted_iota(jnp.int32, (size, size), 1)
    return jnp.where(k <= i, out, 0.0)


def full_col(tile, j, size):
    return jnp.broadcast_to(tile[:, j : j + 1], (8, size))


def inverse_factor(z, group=8, size=128):
    n = z.shape[0]
    blocks = n // size

    def step(k, carry):
        at = pl.ds(pl.multiple_of(k * size, size), size)
        inv = factor_diag(z[at, at], group)
        z[at, :] = jnp.dot(inv, z[at, :], precision=HI, preferred_element_type=f32)
        z[at, at] = inv

        def below(i, c):
            ai = pl.ds(pl.multiple_of(i * size, size), size)
            low = z[at, ai]
            z[ai, at] = jnp.zeros((size, size), f32)
            z[ai, :] = z[ai, :] - lax.dot_general(
                low, z[at, :], (((0,), (0,)), ((), ())), precision=HI, preferred_element_type=f32
            )
            return c

        lax.fori_loop(k + 1, blocks, below, 0)
        return carry

    lax.fori_loop(0, blocks, step, 0)
    row = lax.broadcasted_iota(jnp.int32, (n, n), 0) // size
    col = lax.broadcasted_iota(jnp.int32, (n, n), 1) // size
    z[...] = jnp.where(col <= row, z[...], 0.0)


def chol_kernel(group, a_ref, out_ref):
    out_ref[...] = a_ref[...]
    inverse_factor(out_ref, group)


def inverse_cholesky(gram, group=8, interpret=False):
    n = gram.shape[0]
    return pl.pallas_call(
        functools.partial(chol_kernel, group),
        out_shape=jax.ShapeDtypeStruct((n, n), f32),
        in_specs=[pl.BlockSpec(memory_space=pltpu.VMEM)],
        out_specs=pl.BlockSpec(memory_space=pltpu.VMEM),
        interpret=interpret,
    )(gram)


def local(gradients, test_matrix, old_basis, first_moment, second_moment):
    replica_grad = gradients[0]
    all_first = lax.all_gather(first_moment, ("dp", "row"), axis=0, tiled=True)
    all_second = lax.all_gather(second_moment, ("dp", "row"), axis=0, tiled=True)
    test_values = test_matrix.astype(jnp.bfloat16)
    partial_value = jnp.dot(replica_grad, test_values, preferred_element_type=f32)
    sketch = lax.psum(partial_value, ("dp", "col"))
    both = lax.dot_general(
        sketch,
        jnp.concatenate([sketch, old_basis], axis=1),
        (((0,), (0,)), ((), ())),
        precision=HI,
        preferred_element_type=f32,
    )
    both = lax.psum(both, "row")
    rank = sketch.shape[1]
    inverse = inverse_cholesky(both[:, :rank], 8)
    basis = lax.dot_general(sketch, inverse, (((1,), (1,)), ((), ())), precision=HI, preferred_element_type=f32)
    basis_low = basis.astype(jnp.bfloat16)
    projected = lax.psum_scatter(
        lax.dot_general(basis_low, replica_grad, (((0,), (0,)), ((), ())), preferred_element_type=f32),
        ("dp", "row"),
        scatter_dimension=0,
        tiled=True,
    )
    rank_dev = first_moment.shape[0]
    rank_start = lax.axis_index(("dp", "row")) * rank_dev
    own_inverse = lax.dynamic_slice_in_dim(inverse, rank_start, rank_dev, 0)
    own_rows = jnp.dot(own_inverse, both[:, rank:], precision=HI, preferred_element_type=f32)
    turned_first = jnp.dot(own_rows, all_first, precision=HI, preferred_element_type=f32)
    turned_second = jnp.dot(own_rows * own_rows, all_second, precision=HI, preferred_element_type=f32)
    first_new = 0.9 * turned_first + 0.1 * projected
    second_new = 0.95 * turned_second + 0.05 * projected * projected
    return (projected, first_new, second_new)


def solution(mesh):
    in_specs = (
        P("dp", "row", "col"),
        P("col", None),
        P("row", None),
        P(("dp", "row"), "col"),
        P(("dp", "row"), "col"),
    )
    out_specs = (P(("dp", "row"), "col"), P(("dp", "row"), "col"), P(("dp", "row"), "col"))
    return jax.shard_map(local, mesh=mesh, in_specs=in_specs, out_specs=out_specs, check_vma=False)
```

time: 838 us -> 434 us (0.52)
  other arithmetic: 365 us -> 0 us
  matrix products: 93.3 us -> 48.8 us
  waiting for transfers between devices: 318 us -> 343 us
  Pallas kernels: 0 us -> 23.3 us
  local copies, waits for them, and re-layouts: 24.6 us -> 2.69 us
  between operations: 26.7 us -> 13.8 us
    another operation x62 -> x0, other arithmetic: 358 us -> none  [the longest x45 238 us: local(): jnp.linalg.cholesky(gram_of(upper_factor) + gram_of(partner))]
    all_gather x1, waiting for transfers between devices: 0.01 us -> 52.3 us  [local(): lax.all_gather(second_moment, ('dp', 'row'), axis=0, tiled=True)]
    ppermute x3 -> x0, waiting for transfers between devices: 43.6 us -> none  [from_partner(): lax.ppermute(value, axis, [(i, i ^ 1 << bit) for i in range(lax.axis_size...]
    another operation x31 -> x0, matrix products: 34.7 us -> none  [the longest x18 16.9 us: local(): jnp.linalg.cholesky(gram_of(upper_factor) + gram_of(partner))]
    pallas_call x0 -> x1, Pallas kernels: none -> 23.3 us  [inverse_cholesky(): pl.pallas_call(functools.partial(chol_kernel, group), out_shape=jax.Shape...]
    another operation x29 -> x0, local copies, waits for them, and re-layouts: 14.5 us -> none
    psum x1, waiting for transfers between devices: 55.4 us -> 65.4 us  [local(): both = lax.psum(both, 'row')]
    dot_general x11 -> x6, matrix products: 48.2 us -> 39.6 us  [the longest x1 10.6 us: local(): jnp.dot(replica_grad, test_values, preferred_element_type=f32)]
  transfers between devices with their start and end apart: 8 -> 5, of which waited for: 7 -> 5; matrix products, arithmetic and copies ran while one was open for 3% -> 2% of each run, Pallas kernels for 0% -> 0%
where the time goes in v1:
time: 434 us; the launch traced here: 432 us
  waiting for transfers between devices  343 us (79%)
  matrix products  48.8 us (11%)
  Pallas kernels  23.3 us (5%)
  between operations  13.8 us (3%)
    psum x1, waiting for transfers between devices, local(): sketch = lax.psum(partial_value, ('dp', 'col'))  93.5 us
    reduce_scatter x1, waiting for transfers between devices, local(): lax.psum_scatter(lax.dot_general(basis_low, replica_grad, (((0,), (0,)),...  85.3 us
    psum x1, waiting for transfers between devices, local(): both = lax.psum(both, 'row')  65.4 us
    all_gather x1, waiting for transfers between devices, local(): lax.all_gather(second_moment, ('dp', 'row'), axis=0, tiled=True)  52.3 us
    all_gather x1, waiting for transfers between devices, local(): all_first = lax.all_gather(first_moment, ('dp', 'row'), axis=0, tiled=True)  45.6 us
    pallas_call x1, Pallas kernels, inverse_cholesky(): pl.pallas_call(functools.partial(chol_kernel, group), out_shape=jax.Shape...  23.3 us
    dot_general x1, matrix products, local(): jnp.dot(replica_grad, test_values, preferred_element_type=f32)  10.6 us
    dot_general x1, matrix products, local(): lax.dot_general(sketch, jnp.concatenate([sketch, old_basis], axis=1), (((...  10.1 us
  transfers between devices with their start and end apart: 5, of which 5 were waited for; matrix products, arithmetic and copies ran while one was open for 2% of the time, Pallas kernels for 0%

profile of v1, /device:TPU:0, one launch (start us, length us, event | category | flops | bytes accessed | tf_op | source)
XLA Modules:
  0.0 432.2 jit_solution(9563439355378195727)
XLA Ops:
  7.2 0.0 all-reduce.3.cloned.1.call-start
  7.2 0.0 copy-start.3
  7.2 10.6 %fusion.2 = f32[1024,512]{1,0:T(8,128)} fusion(bf16[1,1024,3584]{2,1,0:T(8,128)(2,1)} %param.5, s32[3584,512]{1,0:T(8,128)} %param.6), kind=kOutput, calls=%fused_computation.2 | convolution fusion | flops 3759931392 | bytes 16777216 | tf_op jit(solution)/shard_map/dot_general | solution.py:108
  17.8 0.0 all-reduce.3.cloned.1.call-update
  17.8 0.0 all-reduce.5.cloned.1.call-start
  17.9 93.5 %all-reduce.3.cloned.1.call-done = f32[1024,512]{1,0:T(8,128)} async-done(((f32[1024,512]{1,0:T(8,128)}), f32[1024,512]{1,0:T(8,128)}) %all-reduce.3.cloned.1.call-update) | async-done | bytes 2097168 | tf_op jit(solution)/shard_map/psum | solution.py:109
  111.4 0.0 copy-done.3
  111.4 10.1 %fusion.6 = f32[512,1024]{1,0:T(8,128)} fusion(f32[1024,512]{1,0:T(8,128)} %all-reduce.3.cloned.1.call-done, f32[1024,512]{1,0:T(8,128)S(1)} %copy-done.3), kind=kOutput, calls=%fused_computation.8 | convolution fusion | flops 6443499520 | bytes 6291456 | tf_op jit(solution)/shard_map/dot_general | solution.py:110
  121.5 0.0 copy-start.1
  121.5 0.0 all-reduce.5.cloned.1.call-update
  121.5 0.2 reduce-scatter.2.cloned.1.call-start
  121.8 65.4 %all-reduce.5.cloned.1.call-done = f32[512,1024]{1,0:T(8,128)} async-done(((f32[512,1024]{1,0:T(8,128)}), f32[512,1024]{1,0:T(8,128)}) %all-reduce.5.cloned.1.call-update) | async-done | bytes 2097168 | tf_op jit(solution)/shard_map/psum | solution.py:117
  187.2 2.3 slice.8.a_ref
  189.4 23.3 %shard_map.76 = f32[512,512]{1,0:T(8,128)} custom-call(f32[512,512]{1,0:T(8,128)} %slice.8.a_ref), custom_call_target="tpu_custom_call" | custom-call | tf_op jit(solution)/shard_map/pallas_call | solution.py:94
  212.8 0.0 copy-done.1
  212.8 4.7 %convolution_convert_fusion = bf16[1024,512]{1,0:T(8,128)(2,1)S(1)} fusion(f32[1024,512]{1,0:T(8,128)S(1)} %copy-done.1, f32[512,512]{1,0:T(8,128)} %shard_map.76), kind=kOutput, calls=%fused_computation.13 | convolution fusion | flops 3221749760 | bytes 4194304 | tf_op jit(solution)/shard_map/dot_general | solution.py:120
  217.5 9.1 %fusion = f32[512,3584]{1,0:T(8,128)} fusion(bf16[1024,512]{1,0:T(8,128)(2,1)S(1)} %convolution_convert_fusion, bf16[1,1024,3584]{2,1,0:T(8,128)(2,1)} %param.5), kind=kOutput, calls=%fused_computation | convolution fusion | flops 3758096384 | bytes 15728640 | tf_op jit(solution)/shard_map/dot_general | solution.py:123
  226.6 0.0 copy-start
  226.6 0.0 reduce-scatter.2.cloned.1.call-update
  226.6 0.0 all-gather.5.cloned.1.call-start
  226.7 0.5 all-gather.5.cloned.1.call-update
  227.2 0.3 all-gather.3.cloned.1.call-start
  227.5 0.3 all-gather.3.cloned.1.call-update
  227.8 0.4 copy-done
  228.2 1.4 fusion.11
  229.6 85.3 %reduce-scatter.2.cloned.1.call-done = f32[16,3584]{1,0:T(8,128)} async-done(((f32[512,3584]{1,0:T(8,128)}), f32[16,3584]{1,0:T(8,128)}) %reduce-scatter.2.cloned.1.call-update) | async-done | bytes 229392 | tf_op jit(solution)/shard_map/reduce_scatter | solution.py:122
  314.9 0.0 copy-start.2
  314.9 52.3 %all-gather.5.cloned.1.call-done = f32[512,3584]{1,0:T(8,128)} async-done(((f32[16,3584]{1,0:T(8,128)}), f32[512,3584]{1,0:T(8,128)}) %all-gather.5.cloned.1.call-update) | async-done | bytes 7340048 | tf_op jit(solution)/shard_map/all_gather | solution.py:106
  367.2 6.4 %fusion.4 = f32[16,3584]{1,0:T(8,128)} fusion(f32[512,3584]{1,0:T(8,128)} %all-gather.5.cloned.1.call-done, f32[16,3584]{1,0:T(8,128)} %reduce-scatter.2.cloned.1.call-done, f32[16,512]{1,0:T(8,128)S(1)} %fusion.11), kind=kOutput, calls=%fused_computation.5 | convolution fusion | flops 352559104 | bytes 7831552 | tf_op jit(solution)/shard_map/dot_general | solution.py:133
  373.6 45.6 %all-gather.3.cloned.1.call-done = f32[512,3584]{1,0:T(8,128)} async-done(((f32[16,3584]{1,0:T(8,128)}), f32[512,3584]{1,0:T(8,128)}) %all-gather.3.cloned.1.call-update) | async-done | bytes 7340048 | tf_op jit(solution)/shard_map/all_gather | solution.py:105
  419.2 0.0 copy-done.2
  419.3 6.4 %fusion.5 = f32[16,3584]{1,0:T(8,128)} fusion(f32[16,512]{1,0:T(8,128)S(1)} %fusion.11, f32[512,3584]{1,0:T(8,128)} %all-gather.3.cloned.1.call-done, f32[16,3584]{1,0:T(8,128)S(1)} %copy-done.2), kind=kOutput, calls=%fused_computation.7 | convolution fusion | flops 352493568 | bytes 7831552 | tf_op jit(solution)/shard_map/dot_general | solution.py:132
Async XLA Ops:
  7.2 104.2 %all-reduce.3.cloned.1.call-start = ((), (), s32[]{:S(2)}) async-start(), calls=%async_computation.1 | async-start | bytes 4194304 | tf_op jit(solution)/shard_map/psum | solution.py:109
  7.2 104.2 %copy-start.3 = (f32[1024,512]{1,0:T(8,128)S(1)}, f32[1024,512]{1,0:T(8,128)}, u32[]{:S(2)}) copy-start(f32[1024,512]{1,0:T(8,128)} %param.7) | copy-start | bytes 6291460
  17.8 169.3 %all-reduce.5.cloned.1.call-start = ((), (), s32[]{:S(2)}) async-start(), calls=%async_computation.2 | async-start | bytes 4194304 | tf_op jit(solution)/shard_map/psum | solution.py:117
  121.5 91.3 %copy-start.1 = (f32[1024,512]{1,0:T(8,128)S(1)}, f32[1024,512]{1,0:T(8,128)}, u32[]{:S(2)}) copy-start(f32[1024,512]{1,0:T(8,128)} %all-reduce.3.cloned.1.call-done) | copy-start | bytes 6291460
  121.5 193.4 %reduce-scatter.2.cloned.1.call-start = ((), (), s32[]{:S(2)}) async-start(), calls=%async_computation.3 | async-start | bytes 7569408 | tf_op jit(solution)/shard_map/reduce_scatter | solution.py:122
  226.6 1.6 copy-start
  226.6 140.6 %all-gather.5.cloned.1.call-start = ((), (), s32[]{:S(2)}) async-start(), calls=%async_computation.5 | async-start | bytes 7569408 | tf_op jit(solution)/shard_map/all_gather | solution.py:106
  227.2 192.0 %all-gather.3.cloned.1.call-start = ((), (), s32[]{:S(2)}) async-start(), calls=%async_computation.4 | async-start | bytes 7569408 | tf_op jit(solution)/shard_map/all_gather | solution.py:105
  314.9 104.4 %copy-start.2 = (f32[16,3584]{1,0:T(8,128)S(1)}, f32[16,3584]{1,0:T(8,128)}, u32[]{:S(2)}) copy-start(f32[16,3584]{1,0:T(8,128)} %reduce-scatter.2.cloned.1.call-done) | copy-start | bytes 688132
Sparse Core Ops, SparseCore 0:
  18.0 93.3 all-reduce.2
  121.7 65.4 all-reduce.4
  226.7 88.0 reduce-scatter.1
  317.0 50.1 all-gather.4
  369.3 49.9 all-gather.2

commit v2 on v1

--- a/solution.py
+++ b/solution.py
@@ -84,65 +84,593 @@
     z[...] = jnp.where(col <= row, z[...], 0.0)
 
 
-def chol_kernel(group, a_ref, out_ref):
-    out_ref[...] = a_ref[...]
-    inverse_factor(out_ref, group)
-
-
-def inverse_cholesky(gram, group=8, interpret=False):
-    n = gram.shape[0]
+MESH = pl.DeviceIdType.MESH
+bf16 = jnp.bfloat16
+SIDE = 4
+
+
+def place():
+    row = lax.axis_index("row")
+    return {"x": lax.axis_index("col"), "y": lax.axis_index("dp"), "z": row // 2, "c": row % 2}
+
+
+def device(at):
+    return (at["y"], at["z"] * 2 + at["c"], at["x"])
+
+
+def moved(at, axis, step):
+    size = 2 if axis == "c" else SIDE
+    return {**at, axis: lax.rem(at[axis] + (step % size), size)}
+
+
+def begin(out):
+    out.start()
+
+
+def sent(out):
+    out.wait_send()
+
+
+def came(out):
+    out.wait_recv()
+
+
+class Links:
+    def __init__(self, at, send, recv):
+        self.at, self.send, self.recv, self.used, self.started = at, send, recv, 0, []
+
+    def copy(self, src, dst, axis, step):
+        i = self.used
+        self.used += 1
+        out = pltpu.make_async_remote_copy(
+            src_ref=src,
+            dst_ref=dst,
+            send_sem=self.send.at[i],
+            recv_sem=self.recv.at[i],
+            device_id=device(moved(self.at, axis, step)),
+            device_id_type=MESH,
+        )
+        out.start()
+        self.started.append(out)
+        return out
+
+    def finish(self):
+        for out in self.started:
+            out.wait_send()
+
+
+def greet(at, near, plane):
+    barrier = pltpu.get_barrier_semaphore()
+    count = 0
+
+    def signal(to):
+        pl.semaphore_signal(barrier, inc=1, device_id=device(to), device_id_type=MESH)
+
+    for axis in near:
+        for step in range(1, 2 if axis == "c" else SIDE):
+            signal(moved(at, axis, step))
+            count += 1
+    if plane:
+        me = at["y"] * 8 + at["z"] * 2 + at["c"]
+
+        def one(step, carry):
+            signal({**at, **plane_place(lax.rem(me + step, 32))})
+            return carry
+
+        lax.fori_loop(1, 32, one, 0)
+        count += 31
+    return barrier, count
+
+
+def plane_place(p):
+    return {"y": p // 8, "z": (p // 2) % 4, "c": p % 2}
+
+
+def tree(own, slots):
+    return (own + slots[1]) + (slots[0] + slots[2])
+
+
+def split3(value):
+    high = value.astype(bf16)
+    rest = value - high.astype(f32)
+    mid = rest.astype(bf16)
+    low = (rest - mid.astype(f32)).astype(bf16)
+    return high, mid, low
+
+
+def sketch_kernel(
+    tiles, g_hbm, t_hbm, o_hbm, m1_ref, m2_ref, gh_ref, s_ref, mc_ref,
+    g_buf, t_buf, t_low, part, half, full, quarter, second, own, o_buf,
+    d_buf, core_in, v0, r1, v1, r2, v2, r3, v3, w1, w0,
+    send, recv, msend, mrecv, local_sem,
+):
+    at = place()
+    x, y, c = at["x"], at["y"], at["c"]
+    me = at["y"] * 8 + at["z"] * 2 + c
+    links = Links(at, send, recv)
+    barrier, count = greet(at, "x", True)
+    first_axis = ("x", "y")
+
+    loads = []
+
+    def load(src, dst):
+        out = pltpu.make_async_copy(src, dst, local_sem.at[len(loads)])
+        out.start()
+        loads.append(out)
+        return out
+
+    steps = (2, 1, -1, 0)
+    chunks = t_buf.shape[0]
+    g_loads, t_loads = {}, {}
+
+    def load_g(i):
+        g_loads[i] = [
+            load(g_hbm.at[colour, lax.rem(at[first_axis[colour]] + steps[i] % SIDE, SIDE)], g_buf.at[i, colour])
+            for colour in range(2)
+        ]
+
+    load_g(0)
+    for k in range(chunks):
+        t_loads[k] = load(t_hbm.at[k], t_buf.at[k])
+    for i in (1, 2, 3):
+        load_g(i)
+    o_loads = [load(o_hbm.at[0, x, y], o_buf.at[0]), load(o_hbm.at[1, y, x], o_buf.at[1])]
+
+    deep = t_buf.shape[1]
+    wide = t_buf.shape[2]
+    rows = g_buf.shape[2]
+
+    def product(i, k):
+        lhs = g_buf[i, :, :, pl.ds(pl.multiple_of(k * deep, deep), deep)].reshape(2 * rows, deep)
+        return jnp.dot(lhs, t_low[k], preferred_element_type=f32).reshape(2, rows, wide)
+
+    def matmul(i):
+        for out in g_loads[i]:
+            out.wait()
+        if i == 0:
+            for k in range(chunks):
+                t_loads[k].wait()
+                t_low[k] = t_buf[k].astype(f32).astype(bf16)
+                part[i] = product(i, k) + (part[i] if k else 0.0)
+        else:
+            part[i] = product(i, 0)
+
+            def more(k, carry):
+                part[i] += product(i, k)
+                return carry
+
+            lax.fori_loop(1, chunks, more, 0)
+
+    def trade(step, moment):
+        to = lax.rem(me + step, 32)
+        col = pl.ds(pl.multiple_of(lax.rem(to, tiles) * 128, 128), 128)
+        return pltpu.make_async_remote_copy(
+            src_ref=(m1_ref, m2_ref)[moment].at[:, col],
+            dst_ref=mc_ref.at[moment, me],
+            send_sem=msend.at[moment, step],
+            recv_sem=mrecv.at[moment, step],
+            device_id=device({**at, **plane_place(to)}),
+            device_id_type=MESH,
+        ), to
+
+    def trade_start(step, carry):
+        for moment in range(2):
+            out, to = trade(step, moment)
+            pl.when(to < tiles)(functools.partial(begin, out))
+        return carry
+
+    def trade_end(step, carry):
+        for moment in range(2):
+            out, to = trade(step, moment)
+            pl.when(to < tiles)(functools.partial(sent, out))
+            pl.when(me < tiles)(functools.partial(came, out))
+        return carry
+
+    matmul(0)
+    pl.semaphore_wait(barrier, count)
+    mid = rows // 2
+    up, down = [], []
+    for colour, axis in enumerate(first_axis):
+        up.append(links.copy(part.at[0, colour, pl.ds(0, mid)], half.at[0, colour], axis, 1))
+        down.append(links.copy(part.at[0, colour, pl.ds(mid, mid)], half.at[1, colour], axis, -1))
+    matmul(1)
+    ups = []
+    for colour, axis in enumerate(first_axis):
+        up[colour].wait_recv()
+        part[1, colour, 0:mid] += half[0, colour]
+        ups.append(links.copy(part.at[1, colour], full.at[0, colour], axis, 1))
+    matmul(2)
+    downs = []
+    for colour, axis in enumerate(first_axis):
+        down[colour].wait_recv()
+        part[2, colour, mid:] += half[1, colour]
+        downs.append(links.copy(part.at[2, colour], full.at[1, colour], axis, -1))
+    matmul(3)
+    later = []
+    for colour, axis in enumerate(first_axis):
+        other = first_axis[1 - colour]
+        ups[colour].wait_recv()
+        downs[colour].wait_recv()
+        total = part[3, colour] + (full[0, colour] + full[1, colour])
+        quarter[colour] = total.reshape(quarter.shape[1:])
+        later.append(
+            [
+                links.copy(
+                    quarter.at[colour, lax.rem(at[other] + step, SIDE)], second.at[colour, step - 1], other, step
+                )
+                for step in (1, 2, 3)
+            ]
+        )
+    for colour in range(2):
+        other = first_axis[1 - colour]
+        for out in later[colour]:
+            out.wait_recv()
+        own[colour] = tree(quarter[colour, at[other]], second[colour])
+
+    gather = []
+    for colour in range(2):
+        other = first_axis[1 - colour]
+        here = s_ref.at[colour, at[first_axis[colour]], at[other]]
+        s_ref[colour, at[first_axis[colour]], at[other]] = own[colour]
+        gather.append([links.copy(own.at[colour], here, other, step) for step in (1, 2, 3)])
+
+    for out in o_loads:
+        out.wait()
+    mine = own[...].reshape(-1, wide)
+    old = o_buf[...].reshape(-1, wide)
+    h, m, l = split3(mine)
+    left = jnp.concatenate([h, h, m, h, m, l], axis=0)
+
+    def share(value):
+        a, b, e = split3(value)
+        right = jnp.concatenate([a, b, a, e, b, a], axis=0)
+        return lax.dot_general(left, right, (((0,), (0,)), ((), ())), preferred_element_type=f32)
+
+    for kind, value in enumerate((mine, old)):
+        for core in range(2):
+            out = share(value[:, core * 256 : core * 256 + 256])
+            for colour in range(2):
+                d_buf[core, colour, kind] = out[:, colour * 128 : colour * 128 + 128].reshape(d_buf.shape[3:])
+    across = links.copy(d_buf.at[1 - c], core_in, "c", 1)
+    lax.fori_loop(1, 32, trade_start, 0)
+
+    @pl.when(me < tiles)
+    def _():
+        col = pl.ds(pl.multiple_of(lax.rem(me, tiles) * 128, 128), 128)
+        mc_ref[0, me] = m1_ref[:, col]
+        mc_ref[1, me] = m2_ref[:, col]
+
+    across.wait_recv()
+    v0[...] = d_buf[c] + core_in[...]
+
+    orders = (("x", "y", "z"), ("y", "z", "x"))
+    pend = [None, None]
+
+    def scatter(buf, slots, level):
+        for colour in range(2):
+            axis = orders[colour][level]
+            pend[colour] = [
+                links.copy(
+                    buf.at[colour, :, lax.rem(at[axis] + step, SIDE)], slots.at[colour, step - 1], axis, step
+                )
+                for step in (1, 2, 3)
+            ]
+
+    def waits():
+        for colour in range(2):
+            for out in pend[colour]:
+                out.wait_recv()
+
+    scatter(v0, r1, 0)
+    ring = []
+    for colour in range(2):
+        axis = first_axis[colour]
+        for out in gather[colour]:
+            out.wait_recv()
+        here = s_ref.at[colour, at[axis]]
+        ring.append((links.copy(here, here, axis, 1), links.copy(here, here, axis, -1)))
+    waits()
+    for colour in range(2):
+        v1[colour] = tree(v0[colour, :, at[orders[colour][0]]], r1[colour]).reshape(v1.shape[1:])
+    scatter(v1, r2, 1)
+    waits()
+    for colour in range(2):
+        v2[colour] = tree(v1[colour, :, at[orders[colour][1]]], r2[colour])
+    for colour in range(2):
+        axis = orders[colour][2]
+        pend[colour] = [links.copy(v2.at[colour], r3.at[colour, step - 1], axis, step) for step in (1, 2, 3)]
+    relay = []
+    for colour in range(2):
+        axis = first_axis[colour]
+        ring[colour][0].wait_recv()
+        ring[colour][1].wait_recv()
+        left_at = lax.rem(at[axis] + 3, SIDE)
+        right_at = lax.rem(at[axis] + 1, SIDE)
+        lo = s_ref.at[colour, left_at, pl.ds(0, 2)]
+        hi = s_ref.at[colour, right_at, pl.ds(2, 2)]
+        relay.append((links.copy(lo, lo, axis, 1), links.copy(hi, hi, axis, -1)))
+    waits()
+    for colour in range(2):
+        v3[colour] = tree(v2[colour], r3[colour])
+    for colour in range(2):
+        axis = orders[colour][1]
+        here = w1.at[colour, :, at[axis]]
+        w1[colour, :, at[axis]] = v3[colour]
+        pend[colour] = [links.copy(v3.at[colour], here, axis, step) for step in (1, 2, 3)]
+    waits()
+    for colour in range(2):
+        axis = orders[colour][0]
+        w0[colour, :, at[axis]] = w1[colour]
+        pend[colour] = [
+            links.copy(w1.at[colour], w0.at[colour, :, at[axis]], axis, step) for step in (1, 2, 3)
+        ]
+    waits()
+    gh_ref[c] = w0[...]
+    last = links.copy(w0, gh_ref.at[c], "c", 1)
+    last.wait_recv()
+    for pair in relay:
+        for out in pair:
+            out.wait_recv()
+    lax.fori_loop(1, 32, trade_end, 0)
+    links.finish()
+
+
+VMEM = pl.BlockSpec(memory_space=pltpu.VMEM)
+ANY = pl.BlockSpec(memory_space=pl.ANY)
+
+
+def sketch_call(grad, test, old, first, second):
+    rows, cols = grad.shape
+    rank = test.shape[1]
+    deep = 512
+    block, small = rows // 8, rows // 32
+    strip = rank // SIDE
+    own_rank, tiles = first.shape[0], cols // 128
+    leg = (2, SIDE, strip, 128)
+    leg2 = (2, SIDE, strip // SIDE, 128)
+    whole = (2, SIDE, SIDE, strip // SIDE, 128)
+    buf = lambda *shape: pltpu.VMEM(shape, f32)
     return pl.pallas_call(
-        functools.partial(chol_kernel, group),
-        out_shape=jax.ShapeDtypeStruct((n, n), f32),
-        in_specs=[pl.BlockSpec(memory_space=pltpu.VMEM)],
-        out_specs=pl.BlockSpec(memory_space=pltpu.VMEM),
-        interpret=interpret,
-    )(gram)
+        functools.partial(sketch_kernel, tiles),
+        out_shape=(
+            jax.ShapeDtypeStruct((2, 2) + whole, f32),
+            jax.ShapeDtypeStruct((2, SIDE, SIDE, small, rank), f32),
+            jax.ShapeDtypeStruct((2, 32, own_rank, 128), f32),
+        ),
+        in_specs=[ANY, ANY, ANY, VMEM, VMEM],
+        out_specs=(VMEM, VMEM, VMEM),
+        scratch_shapes=[
+            pltpu.VMEM((4, 2, block, cols), bf16),
+            pltpu.VMEM((cols // deep, deep, rank), jnp.int32),
+            pltpu.VMEM((cols // deep, deep, rank), bf16),
+            buf(4, 2, block, rank),
+            buf(2, 2, block // 2, rank),
+            buf(2, 2, block, rank),
+            buf(2, SIDE, small, rank),
+            buf(2, 3, small, rank),
+            buf(2, small, rank),
+            buf(2, small, rank),
+            buf(2, 2, *leg),
+            buf(2, *leg),
+            buf(2, *leg),
+            buf(2, 3, 2, strip, 128),
+            buf(2, *leg2),
+            buf(2, 3, 2, strip // SIDE, 128),
+            buf(2, 2, strip // SIDE, 128),
+            buf(2, 3, 2, strip // SIDE, 128),
+            buf(2, 2, strip // SIDE, 128),
+            buf(2, *leg2),
+            buf(2, *whole),
+            pltpu.SemaphoreType.DMA((64,)),
+            pltpu.SemaphoreType.DMA((64,)),
+            pltpu.SemaphoreType.DMA((2, 32)),
+            pltpu.SemaphoreType.DMA((2, 32)),
+            pltpu.SemaphoreType.DMA((32,)),
+        ],
+        compiler_params=pltpu.CompilerParams(collective_id=0, has_side_effects=True),
+    )(
+        grad.reshape(2, SIDE, block, cols),
+        test.reshape(cols // deep, deep, rank),
+        old.reshape(2, SIDE, SIDE, small, rank),
+        first,
+        second,
+    )
+
+
+def factor_kernel(gh_ref, mc_ref, inv_ref, turned_ref):
+    size = 128
+    rank = inv_ref.shape[0]
+    for part in range(rank // size):
+        inv_ref[:, part * size : part * size + size] = gh_ref[part // 2, part % 2, 0].reshape(rank, size)
+    inverse_factor(inv_ref)
+    inverse = inv_ref[...]
+    mixed = jnp.concatenate([gh_ref[p // 2, p % 2, 1].reshape(rank, size) for p in range(rank // size)], axis=1)
+    corr = jnp.dot(inverse, mixed, precision=HI, preferred_element_type=f32)
+    shape = turned_ref.shape[1:]
+    old = mc_ref[0].reshape(rank, size)
+    turned_ref[0] = jnp.dot(corr, old, precision=HI, preferred_element_type=f32).reshape(shape)
+    old = mc_ref[1].reshape(rank, size)
+    turned_ref[1] = jnp.dot(corr * corr, old, precision=HI, preferred_element_type=f32).reshape(shape)
+
+
+def factor_call(gh, mc):
+    rank = mc.shape[1] * mc.shape[2]
+    return pl.pallas_call(
+        factor_kernel,
+        out_shape=(jax.ShapeDtypeStruct((rank, rank), f32), jax.ShapeDtypeStruct(mc.shape, f32)),
+        in_specs=[VMEM, VMEM],
+        out_specs=(VMEM, VMEM),
+    )(gh, mc)
+
+
+LAGS = (1, 2, 3, 4)
+
+
+def project_kernel(
+    tiles, bt_ref, g_hbm, turned_ref, proj_ref, first_ref, second_ref,
+    g_buf, x_buf, core_in, y_buf, r_half, r_full, t_buf, last, t_in,
+    send, recv, tsend, trecv, local_sem,
+):
+    at = place()
+    c = at["c"]
+    me = at["y"] * 8 + at["z"] * 2 + c
+    links = Links(at, send, recv)
+    barrier, count = greet(at, "", True)
+    blocks = g_buf.shape[0]
+    wide = g_buf.shape[2]
+    cut = wide // 2
+    axes = (("y", "z"), ("z", "y"))
+
+    loads = []
+    for b in range(blocks):
+        out = pltpu.make_async_copy(g_hbm.at[:, pl.ds(b * wide, wide)], g_buf.at[b], local_sem.at[b])
+        out.start()
+        loads.append(out)
+
+    def give(step):
+        to, source = lax.rem(me + step, 32), lax.rem(me + (32 - step), 32)
+        col = pl.ds(pl.multiple_of(lax.rem(me, tiles) * 128, 128), 128)
+        return pltpu.make_async_remote_copy(
+            src_ref=turned_ref.at[:, to],
+            dst_ref=t_in.at[:, :, col],
+            send_sem=tsend.at[step],
+            recv_sem=trecv.at[step],
+            device_id=device({**at, **plane_place(to)}),
+            device_id_type=MESH,
+        ), source
+
+    def give_start(step, carry):
+        out, source = give(step)
+        pl.when(me < tiles)(functools.partial(begin, out))
+        return carry
+
+    def give_end(step, carry):
+        out, source = give(step)
+        pl.when(me < tiles)(functools.partial(sent, out))
+        pl.when(source < tiles)(functools.partial(came, out))
+        return carry
+
+    across, firsts, fulls, lasts = {}, {}, {}, {}
+
+    def multiply(b):
+        loads[b].wait()
+        out = jnp.dot(bt_ref[...], g_buf[b], preferred_element_type=f32)
+        x_buf[b] = out.reshape(x_buf.shape[1:])
+        if b == 0:
+            pl.semaphore_wait(barrier, count)
+        across[b] = links.copy(x_buf.at[b, :, :, 1 - c], core_in.at[b], "c", 1)
+
+    def start_ring(b):
+        across[b].wait_recv()
+        total = x_buf[b, :, :, c] + core_in[b]
+        y_buf[b, 0] = total[..., :cut]
+        for i in range(SIDE):
+            y_buf[b, 1, :, i] = total[i, :, :, cut:]
+        for colour in range(2):
+            axis = axes[colour][0]
+            far = lax.rem(at[axis] + 2, SIDE)
+            firsts[b, colour] = (
+                links.copy(y_buf.at[b, colour, far, pl.ds(0, 2)], r_half.at[b, colour, 0], axis, 1),
+                links.copy(y_buf.at[b, colour, far, pl.ds(2, 2)], r_half.at[b, colour, 1], axis, -1),
+            )
+
+    def pass_on(b):
+        for colour in range(2):
+            axis = axes[colour][0]
+            outs = []
+            for side in range(2):
+                firsts[b, colour][side].wait_recv()
+                to = lax.rem(at[axis] + (1, 3)[side], SIDE)
+                y_buf[b, colour, to, 2 * side : 2 * side + 2] += r_half[b, colour, side]
+                outs.append(links.copy(y_buf.at[b, colour, to], r_full.at[b, colour, side], axis, (1, -1)[side]))
+            fulls[b, colour] = outs
+
+    def second_axis(b):
+        for colour in range(2):
+            axis, other = axes[colour]
+            for out in fulls[b, colour]:
+                out.wait_recv()
+            t_buf[b, colour] = y_buf[b, colour, at[axis]] + (r_full[b, colour, 0] + r_full[b, colour, 1])
+            lasts[b, colour] = [
+                links.copy(
+                    t_buf.at[b, colour, lax.rem(at[other] + step, SIDE)], last.at[b, colour, step - 1], other, step
+                )
+                for step in (1, 2, 3)
+            ]
+
+    def complete(b):
+        for colour in range(2):
+            for out in lasts[b, colour]:
+                out.wait_recv()
+            start = b * wide + colour * cut
+            proj_ref[:, start : start + cut] = tree(t_buf[b, colour, at[axes[colour][1]]], last[b, colour])
+
+    jobs = (start_ring, pass_on, second_axis, complete)
+    for tick in range(blocks + LAGS[-1]):
+        if tick < blocks:
+            multiply(tick)
+        if tick == 0:
+            lax.fori_loop(1, 32, give_start, 0)
+        for job, lag in reversed(tuple(zip(jobs, LAGS))):
+            if 0 <= tick - lag < blocks:
+                job(tick - lag)
+
+    @pl.when(me < tiles)
+    def _():
+        col = pl.ds(pl.multiple_of(lax.rem(me, tiles) * 128, 128), 128)
+        t_in[:, :, col] = turned_ref[:, me]
+
+    lax.fori_loop(1, 32, give_end, 0)
+    total = proj_ref[...]
+    first_ref[...] = 0.9 * t_in[0] + 0.1 * total
+    second_ref[...] = 0.95 * t_in[1] + 0.05 * total * total
+    links.finish()
+
+
+def project_call(bt, grad, turned):
+    rank, rows = bt.shape
+    cols = grad.shape[1]
+    own = turned.shape[2]
+    wide = 512
+    blocks = cols // wide
+    cut = wide // 2
+    out = jax.ShapeDtypeStruct((own, cols), f32)
+    buf = lambda *shape: pltpu.VMEM(shape, f32)
+    return pl.pallas_call(
+        functools.partial(project_kernel, cols // 128),
+        out_shape=(out, out, out),
+        in_specs=[VMEM, ANY, VMEM],
+        out_specs=(VMEM, VMEM, VMEM),
+        scratch_shapes=[
+            pltpu.VMEM((blocks, rows, wide), bf16),
+            buf(blocks, SIDE, SIDE, 2, own, wide),
+            buf(blocks, SIDE, SIDE, own, wide),
+            buf(blocks, 2, SIDE, SIDE, own, cut),
+            buf(blocks, 2, 2, 2, own, cut),
+            buf(blocks, 2, 2, SIDE, own, cut),
+            buf(blocks, 2, SIDE, own, cut),
+            buf(blocks, 2, 3, own, cut),
+            buf(2, own, cols),
+            pltpu.SemaphoreType.DMA((15 * blocks,)),
+            pltpu.SemaphoreType.DMA((15 * blocks,)),
+            pltpu.SemaphoreType.DMA((32,)),
+            pltpu.SemaphoreType.DMA((32,)),
+            pltpu.SemaphoreType.DMA((blocks,)),
+        ],
+        compiler_params=pltpu.CompilerParams(collective_id=1, has_side_effects=True),
+    )(bt, grad, turned)
 
 
 def local(gradients, test_matrix, old_basis, first_moment, second_moment):
-    replica_grad = gradients[0]
-    all_first = lax.all_gather(first_moment, ("dp", "row"), axis=0, tiled=True)
-    all_second = lax.all_gather(second_moment, ("dp", "row"), axis=0, tiled=True)
-    test_values = test_matrix.astype(jnp.bfloat16)
-    partial_value = jnp.dot(replica_grad, test_values, preferred_element_type=f32)
-    sketch = lax.psum(partial_value, ("dp", "col"))
-    both = lax.dot_general(
-        sketch,
-        jnp.concatenate([sketch, old_basis], axis=1),
-        (((0,), (0,)), ((), ())),
-        precision=HI,
-        preferred_element_type=f32,
-    )
-    both = lax.psum(both, "row")
-    rank = sketch.shape[1]
-    inverse = inverse_cholesky(both[:, :rank], 8)
-    basis = lax.dot_general(sketch, inverse, (((1,), (1,)), ((), ())), precision=HI, preferred_element_type=f32)
-    basis_low = basis.astype(jnp.bfloat16)
-    projected = lax.psum_scatter(
-        lax.dot_general(basis_low, replica_grad, (((0,), (0,)), ((), ())), preferred_element_type=f32),
-        ("dp", "row"),
-        scatter_dimension=0,
-        tiled=True,
-    )
-    rank_dev = first_moment.shape[0]
-    rank_start = lax.axis_index(("dp", "row")) * rank_dev
-    own_inverse = lax.dynamic_slice_in_dim(inverse, rank_start, rank_dev, 0)
-    own_rows = jnp.dot(own_inverse, both[:, rank:], precision=HI, preferred_element_type=f32)
-    turned_first = jnp.dot(own_rows, all_first, precision=HI, preferred_element_type=f32)
-    turned_second = jnp.dot(own_rows * own_rows, all_second, precision=HI, preferred_element_type=f32)
-    first_new = 0.9 * turned_first + 0.1 * projected
-    second_new = 0.95 * turned_second + 0.05 * projected * projected
-    return (projected, first_new, second_new)
+    grad = gradients[0]
+    gh, sketch, columns = sketch_call(grad, test_matrix, old_basis, first_moment, second_moment)
+    inverse, turned = factor_call(gh, columns)
+    sketch = sketch.reshape(grad.shape[0], -1)
+    basis = lax.dot_general(inverse, sketch, (((1,), (1,)), ((), ())), precision=HI, preferred_element_type=f32)
+    return project_call(basis.astype(bf16), grad, turned)
 
 
 def solution(mesh):
-    in_specs = (
-        P("dp", "row", "col"),
-        P("col", None),
-        P("row", None),
-        P(("dp", "row"), "col"),
-        P(("dp", "row"), "col"),
-    )
-    out_specs = (P(("dp", "row"), "col"), P(("dp", "row"), "col"), P(("dp", "row"), "col"))
-    return jax.shard_map(local, mesh=mesh, in_specs=in_specs, out_specs=out_specs, check_vma=False)
+    moment = P(("dp", "row"), "col")
+    in_specs = (P("dp", "row", "col"), P("col", None), P("row", None), moment, moment)
+    return jax.shard_map(local, mesh=mesh, in_specs=in_specs, out_specs=(moment,) * 3, check_vma=False)

time: 434 us -> 168 us (0.39)
  waiting for transfers between devices: 343 us -> 0 us
  Pallas kernels: 23.3 us -> 156 us
  matrix products: 48.8 us -> 5.76 us
  between operations: 13.8 us -> 0.66 us
    psum x2 -> x0, waiting for transfers between devices: 159 us -> none  [the longest x1 93.5 us: local(): sketch = lax.psum(partial_value, ('dp', 'col'))]
    pallas_call x1 -> x3, Pallas kernels: 23.3 us -> 156 us  [the longest x1 74.7 us: sketch_call(): pl.pallas_call(functools.partial(sketch_kernel, tiles), out_shape=(jax.Sh...]
    all_gather x2 -> x0, waiting for transfers between devices: 97.9 us -> none  [the longest x1 52.3 us: local(): lax.all_gather(second_moment, ('dp', 'row'), axis=0, tiled=True)]
    reduce_scatter x1 -> x0, waiting for transfers between devices: 85.3 us -> none  [local(): lax.psum_scatter(lax.dot_general(basis_low, replica_grad, (((0,), (0,)),...]
    dot_general x7 -> x1, matrix products: 48.8 us -> 5.76 us  [local(): lax.dot_general(inverse, sketch, (((1,), (1,)), ((), ())), precision=HI,...]
    unnamed x8 -> x5, local copies, waits for them, and re-layouts: 0.4 us -> 4.93 us
  transfers between devices with their start and end apart: 5 -> 0, of which waited for: 5 -> 0; matrix products, arithmetic and copies ran while one was open for 2% -> 0% of each run, Pallas kernels for 0% -> 0%
where the time goes in v2:
time: 168 us; the launch traced here: 167 us
  Pallas kernels  156 us (93%)
  matrix products  5.76 us (3%)
  local copies, waits for them, and re-layouts  4.93 us (3%)
    pallas_call x1, Pallas kernels, sketch_call(): pl.pallas_call(functools.partial(sketch_kernel, tiles), out_shape=(jax.Sh...  74.7 us
    pallas_call x1, Pallas kernels, project_call(): pl.pallas_call(functools.partial(project_kernel, cols // 128), out_shape=...  53.9 us
    pallas_call x1, Pallas kernels, factor_call(): pl.pallas_call(factor_kernel, out_shape=(jax.ShapeDtypeStruct((rank, rank...  27.6 us
    dot_general x1, matrix products, local(): lax.dot_general(inverse, sketch, (((1,), (1,)), ((), ())), precision=HI,...  5.76 us
    unnamed x5, local copies, waits for them, and re-layouts  4.93 us

profile of v2, /device:TPU:0, one launch (start us, length us, event | category | flops | bytes accessed | tf_op | source)
XLA Modules:
  0.0 167.4 jit_solution(10430137890464993727)
XLA Ops:
  0.6 74.7 %shard_map.76 = (f32[2,2,2,4,4,32,128]{6,5,4,3,2,1,0:T(8,128)}, f32[2,4,4,32,512]{4,3,2,1,0:T(8,128)}, f32[2,32,16,128]{3,2,1,0:T(8,128)}) custom-call(bf16[2,4,128,3584]{3,2,1,0:T(8,128)(2,1)} %bitcast.7, s32[7,512,512]{2,1,0:T(8,128)} %bitcast.9, f32[2,4,4,32,512]{4,3,2,1,0:T(8,128)} %bitcast.10, f32[16,3584]{1,0:T(8,128)} %m1_ref.1, f32[16,3584]{1,0:T(8,128)} %m2_ref.1), custom_call_target="tpu_custom_call" | custom-call | tf_op jit(solution)/shard_map/pallas_call | solution.py:433
  75.3 0.0 copy-start
  75.3 27.6 %shard_map.77 = (f32[512,512]{1,0:T(8,128)}, f32[2,32,16,128]{3,2,1,0:T(8,128)}) custom-call(f32[2,2,2,4,4,32,128]{6,5,4,3,2,1,0:T(8,128)} %get-tuple-element.8.gh_ref, f32[2,32,16,128]{3,2,1,0:T(8,128)} %get-tuple-element.9.mc_ref), custom_call_target="tpu_custom_call" | custom-call | tf_op jit(solution)/shard_map/pallas_call | solution.py:498
  102.9 0.0 copy-done
  102.9 5.8 %convolution_convert_fusion.bt_ref = bf16[512,1024]{1,0:T(8,128)(2,1)} fusion(f32[512,512]{1,0:T(8,128)} %get-tuple-element.10, f32[1024,512]{1,0:T(8,128)S(1)} %bitcast.11), kind=kOutput, calls=%fused_computation | convolution fusion | flops 3221749760 | bytes 4194304 | tf_op jit(solution)/shard_map/dot_general | solution.py:669
  108.6 53.9 %shard_map.78 = (f32[16,3584]{1,0:T(8,128)}, f32[16,3584]{1,0:T(8,128)}, f32[16,3584]{1,0:T(8,128)}) custom-call(bf16[512,1024]{1,0:T(8,128)(2,1)} %convolution_convert_fusion.bt_ref, bf16[1024,3584]{1,0:T(8,128)(2,1)} %bitcast.8, f32[2,32,16,128]{3,2,1,0:T(8,128)} %get-tuple-element.12.turned_ref), custom_call_target="tpu_custom_call" | custom-call | tf_op jit(solution)/shard_map/pallas_call | solution.py:639
  162.5 1.6 copy.11
  164.2 1.6 copy.12
  165.8 1.6 copy.13
Async XLA Ops:
  75.3 27.6 %copy-start = (f32[2,4,4,32,512]{4,3,2,1,0:T(8,128)S(1)}, f32[2,4,4,32,512]{4,3,2,1,0:T(8,128)}, u32[]{:S(2)}) copy-start(f32[2,4,4,32,512]{4,3,2,1,0:T(8,128)} %get-tuple-element.11) | copy-start | bytes 6291460

commit v3 on v1

v3 whole, which is shorter than its diff:
```python
import functools
import jax, jax.numpy as jnp
from jax import lax
from jax.experimental import pallas as pl
from jax.experimental.pallas import tpu as pltpu
from jax.sharding import PartitionSpec as P

HI = lax.Precision.HIGHEST
f32 = jnp.float32


def factor_diag(block, group):
    size = block.shape[0]
    tiles = size // 8
    z = [block[8 * b : 8 * b + 8, :] for b in range(tiles)]
    lane = lax.broadcasted_iota(jnp.int32, (8, size), 1)
    sub = lax.broadcasted_iota(jnp.int32, (8, size), 0)
    full = lambda v: jnp.broadcast_to(v, (8, size))
    for b in range(tiles):
        pivots = jnp.ones((8, size), f32)
        for r in range(0, 8, group):
            j = 8 * b + r
            piv = [[full(z[b][r + t : r + t + 1, j + s : j + s + 1]) for s in range(group)] for t in range(group)]
            inside = (lane >= j) & (lane < j + group)
            rows = [
                jnp.where(inside, (lane == j + t).astype(f32), full(z[b][r + t : r + t + 1, :])) for t in range(group)
            ]
            inv = []
            for t in range(group):
                pivots = jnp.where(sub == r + t, piv[t][t], pivots)
                inv.append(1.0 / piv[t][t])
                for u in range(t + 1, group):
                    m = piv[t][u] * inv[t]
                    for s in range(u, group):
                        piv[u][s] = piv[u][s] - m * piv[t][s]
                    rows[u] = rows[u] - m * rows[t]
            for i in range(b, tiles):
                cols = [full_col(z[i], j + t, size) for t in range(group)]
                acc = jnp.where(inside, (sub - r == lane - j).astype(f32) if i == b else 0.0, z[i])
                for t in range(group):
                    m = cols[t] * inv[t]
                    for u in range(t + 1, group):
                        cols[u] = cols[u] - m * piv[t][u]
                    if i == b:
                        m = jnp.where(sub > r + t, m, 0.0)
                    acc = acc - m * rows[t]
                z[i] = acc
        z[b] = z[b] * lax.rsqrt(pivots)
    out = jnp.concatenate(z, axis=0)
    i = lax.broadcasted_iota(jnp.int32, (size, size), 0)
    k = lax.broadcasted_iota(jnp.int32, (size, size), 1)
    return jnp.where(k <= i, out, 0.0)


def full_col(tile, j, size):
    return jnp.broadcast_to(tile[:, j : j + 1], (8, size))


def inverse_factor(z, group=8, size=128, ticks=()):
    n = z.shape[0]
    blocks = n // size
    for k in range(blocks):
        at = slice(k * size, k * size + size)
        inv = factor_diag(z[at, at], group)
        z[at, :] = jnp.dot(inv, z[at, :], precision=HI, preferred_element_type=f32)
        z[at, at] = inv
        if 2 * k < len(ticks):
            ticks[2 * k]()
        if k + 1 < blocks:
            below = slice(k * size + size, n)
            low = z[at, below]
            z[below, at] = jnp.zeros((n - below.start, size), f32)
            z[below, :] = z[below, :] - lax.dot_general(
                low, z[at, :], (((0,), (0,)), ((), ())), precision=HI, preferred_element_type=f32
            )
        if 2 * k + 1 < len(ticks):
            ticks[2 * k + 1]()
    row = lax.broadcasted_iota(jnp.int32, (n, n), 0) // size
    col = lax.broadcasted_iota(jnp.int32, (n, n), 1) // size
    z[...] = jnp.where(col <= row, z[...], 0.0)
MESH = pl.DeviceIdType.MESH
bf16 = jnp.bfloat16
SIDE = 4
VMEM = pl.BlockSpec(memory_space=pltpu.VMEM)
ANY = pl.BlockSpec(memory_space=pl.ANY)
LAGS = (1, 3, 5, 7)
TURN = 3


def plane_place(p):
    return {"y": p // 8, "z": (p // 2) % 4, "c": p % 2}


def device(at):
    return (at["y"], at["z"] * 2 + at["c"], at["x"])


class Place:
    def __init__(self):
        row = lax.axis_index("row")
        self.at = {"x": lax.axis_index("col"), "y": lax.axis_index("dp"), "z": row // 2, "c": row % 2}
        self.rank = self.at["y"] * 8 + row
        self.near, self.devices = {}, {}
        for axis, here in self.at.items():
            size = 2 if axis == "c" else SIDE
            for step in range(size):
                there = lax.rem(here + step, size)
                self.near[axis, step] = there
                self.devices[axis, step] = device({**self.at, axis: there})

    def __getitem__(self, axis):
        return self.at[axis]

    def of(self, axis, step):
        return self.near[axis, step % SIDE]


class Copy:
    def __init__(self, links, src, dst, axis, step, number):
        self.links, self.src, self.dst, self.number = links, src, dst, number
        self.device = links.place.devices[axis, step % (2 if axis == "c" else SIDE)]

    def build(self):
        src, dst = (ref[0].at[ref[1]] if isinstance(ref, tuple) else ref for ref in (self.src, self.dst))
        return pltpu.make_async_remote_copy(
            src_ref=src,
            dst_ref=dst,
            send_sem=self.links.send.at[self.number],
            recv_sem=self.links.recv.at[self.number],
            device_id=self.device,
            device_id_type=MESH,
        )

    def wait_recv(self):
        self.build().wait_recv()

    def wait_send(self):
        self.build().wait_send()


class Links:
    def __init__(self, place, send, recv):
        self.place, self.send, self.recv, self.used, self.started = place, send, recv, 0, []

    def copy(self, src, dst, axis, step):
        out = Copy(self, src, dst, axis, step, self.used)
        self.used += 1
        self.started.append(out)
        out.build().start()
        return out

    def finish(self):
        for out in self.started:
            out.wait_send()


def begin(out):
    out.start()


def sent(out):
    out.wait_send()


def came(out):
    out.wait_recv()


def arrive(outs):
    for out in outs:
        out.wait_recv()


def tree(own, slots):
    return (own + slots[1]) + (slots[0] + slots[2])


def split3(value):
    high = value.astype(bf16)
    rest = value - high.astype(f32)
    mid = rest.astype(bf16)
    low = (rest - mid.astype(f32)).astype(bf16)
    return high, mid, low


class Total:
    orders = (("x", "y", "z"), ("y", "z", "x"))

    def __init__(self, place, links, parts, core_in, v0, r1, v1, r2, v2, r3, v3, w1, w0, out):
        self.place, self.links, self.parts, self.core_in, self.out = place, links, parts, core_in, out
        self.v0, self.r1, self.v1, self.r2, self.v2 = v0, r1, v1, r2, v2
        self.r3, self.v3, self.w1, self.w0 = r3, v3, w1, w0
        self.flying = []

    def steps(self):
        return (self.core, self.first, self.second, self.third, self.back2, self.back1, self.join, self.end)

    def core(self):
        self.flying = [self.links.copy(self.parts.at[1 - self.place["c"]], self.core_in, "c", 1)]

    def send(self, level, src, dst):
        arrivals = []
        for colour in range(2):
            axis = self.orders[colour][level]
            for step in (1, 2, 3):
                arrivals.append(self.links.copy(src(colour, axis, step), dst(colour, axis, step), axis, step))
        self.flying = arrivals

    def first(self):
        arrive(self.flying)
        self.v0[...] = self.parts[self.place["c"]] + self.core_in[...]
        self.send(
            0,
            lambda colour, axis, step: self.v0.at[colour, self.place.of(axis, step)],
            lambda colour, axis, step: self.r1.at[colour, step - 1],
        )

    def second(self):
        arrive(self.flying)
        for colour in range(2):
            mine = self.v0[colour, self.place[self.orders[colour][0]]]
            self.v1[colour] = tree(mine, self.r1[colour]).reshape(self.v1.shape[1:])
        self.send(
            1,
            lambda colour, axis, step: self.v1.at[colour, self.place.of(axis, step)],
            lambda colour, axis, step: self.r2.at[colour, step - 1],
        )

    def third(self):
        arrive(self.flying)
        for colour in range(2):
            self.v2[colour] = tree(self.v1[colour, self.place[self.orders[colour][1]]], self.r2[colour])
        self.send(
            2,
            lambda colour, axis, step: self.v2.at[colour],
            lambda colour, axis, step: self.r3.at[colour, step - 1],
        )

    def back2(self):
        arrive(self.flying)
        for colour in range(2):
            total = tree(self.v2[colour], self.r3[colour])
            self.v3[colour] = total
            self.w1[colour, self.place[self.orders[colour][1]]] = total
        self.send(
            1,
            lambda colour, axis, step: self.v3.at[colour],
            lambda colour, axis, step: self.w1.at[colour, self.place[axis]],
        )

    def back1(self):
        arrive(self.flying)
        for colour in range(2):
            self.w0[colour, self.place[self.orders[colour][0]]] = self.w1[colour]
        self.send(
            0,
            lambda colour, axis, step: self.w1.at[colour],
            lambda colour, axis, step: self.w0.at[colour, self.place[axis]],
        )

    def join(self):
        arrive(self.flying)
        c = self.place["c"]
        self.out[c] = self.w0[...]
        self.flying = [self.links.copy(self.w0, self.out.at[c], "c", 1)]

    def end(self):
        arrive(self.flying)


def kernel(
    tiles, g_hbm, t_hbm, o_hbm, m1_ref, m2_ref, pa_ref, pb_ref, tin_ref,
    g_buf, t_buf, t_low, part, half, full, quarter, second, own, o_buf,
    parts, core_in, v0, r1, v1, r2, v2, r3, v3, w1, w0, totals,
    s_buf, mc_buf, z_buf, turned, b_low,
    x_buf, x_in, y_buf, r_half, r_full, p_buf, p_in,
    send, recv, msend, mrecv, tsend, trecv, local_sem,
):
    place = Place()
    x, y, c, me = place["x"], place["y"], place["c"], place.rank
    links = Links(place, send, recv)
    first_axis = ("x", "y")

    barrier = pltpu.get_barrier_semaphore()

    def greet(step, carry):
        to = {**place.at, **plane_place(lax.rem(me + step, 32))}
        pl.semaphore_signal(barrier, inc=1, device_id=device(to), device_id_type=MESH)
        return carry

    for step in (1, 2, 3):
        pl.semaphore_signal(barrier, inc=1, device_id=place.devices["x", step], device_id_type=MESH)
    lax.fori_loop(1, 32, greet, 0)

    loads = []

    def load(src, dst):
        out = pltpu.make_async_copy(src, dst, local_sem.at[len(loads)])
        out.start()
        loads.append(out)
        return out

    steps = (2, 1, -1, 0)
    chunks, deep, wide = t_buf.shape
    rows = g_buf.shape[2]
    g_loads, t_loads = {}, {}

    def load_g(i):
        g_loads[i] = [
            load(g_hbm.at[colour, place.of(first_axis[colour], steps[i])], g_buf.at[i, colour]) for colour in range(2)
        ]

    load_g(0)
    for k in range(chunks):
        t_loads[k] = load(t_hbm.at[k], t_buf.at[k])
    for i in (1, 2, 3):
        load_g(i)
    o_loads = [load(o_hbm.at[0, x, y], o_buf.at[0]), load(o_hbm.at[1, y, x], o_buf.at[1])]

    def product(i, k):
        lhs = g_buf[i, :, :, pl.ds(pl.multiple_of(k * deep, deep), deep)].reshape(2 * rows, deep)
        return jnp.dot(lhs, t_low[k], preferred_element_type=f32).reshape(2, rows, wide)

    def matmul(i):
        for out in g_loads[i]:
            out.wait()
        if i == 0:
            for k in range(chunks):
                t_loads[k].wait()
                t_low[k] = t_buf[k].astype(f32).astype(bf16)
                part[i] = product(i, k) + (part[i] if k else 0.0)
        else:
            part[i] = product(i, 0)

            def more(k, carry):
                part[i] += product(i, k)
                return carry

            lax.fori_loop(1, chunks, more, 0)

    matmul(0)
    pl.semaphore_wait(barrier, 34)
    mid = rows // 2
    up, down, ups, downs, later = [], [], [], [], []
    for colour, axis in enumerate(first_axis):
        up.append(links.copy(part.at[0, colour, pl.ds(0, mid)], half.at[0, colour], axis, 1))
        down.append(links.copy(part.at[0, colour, pl.ds(mid, mid)], half.at[1, colour], axis, -1))
    matmul(1)
    for colour, axis in enumerate(first_axis):
        up[colour].wait_recv()
        part[1, colour, 0:mid] += half[0, colour]
        ups.append(links.copy(part.at[1, colour], full.at[0, colour], axis, 1))
    matmul(2)
    for colour, axis in enumerate(first_axis):
        down[colour].wait_recv()
        part[2, colour, mid:] += half[1, colour]
        downs.append(links.copy(part.at[2, colour], full.at[1, colour], axis, -1))
    matmul(3)
    for colour, axis in enumerate(first_axis):
        other = first_axis[1 - colour]
        arrive((ups[colour], downs[colour]))
        total = part[3, colour] + (full[0, colour] + full[1, colour])
        quarter[colour] = total.reshape(quarter.shape[1:])
        later.append(
            [
                links.copy(quarter.at[colour, place.of(other, step)], second.at[colour, step - 1], other, step)
                for step in (1, 2, 3)
            ]
        )
    for colour in range(2):
        arrive(later[colour])
        own[colour] = tree(quarter[colour, place[first_axis[1 - colour]]], second[colour])

    mine = own[...].reshape(-1, wide)
    h, m, l = split3(mine)
    left = jnp.concatenate([h, h, m, h, m, l], axis=0)

    def share(value, kind):
        for core in range(2):
            a, b, e = split3(value[:, core * 256 : core * 256 + 256])
            right = jnp.concatenate([a, b, a, e, b, a], axis=0)
            out = lax.dot_general(left, right, (((0,), (0,)), ((), ())), preferred_element_type=f32)
            for colour in range(2):
                parts[kind, core, colour] = out[:, colour * 128 : colour * 128 + 128].reshape(parts.shape[3:])

    grams, mixes = (
        Total(
            place, links, parts.at[kind], core_in.at[kind], v0.at[kind], r1.at[kind], v1.at[kind], r2.at[kind],
            v2.at[kind], r3.at[kind], v3.at[kind], w1.at[kind], w0.at[kind], totals.at[kind],
        )
        for kind in range(2)
    )
    share(mine, 0)
    grams.core()
    for out in o_loads:
        out.wait()
    share(o_buf[...].reshape(-1, wide), 1)
    grams.first()
    mixes.core()
    grams.second()
    grams.third()
    grams.back2()
    grams.back1()
    grams.join()

    gather, ring, relay = [], [], []

    def gather_first():
        for colour in range(2):
            axis, other = first_axis[colour], first_axis[1 - colour]
            s_buf[colour, place[axis], place[other]] = own[colour]
            here = s_buf.at[colour, place[axis], place[other]]
            gather.extend(links.copy(own.at[colour], here, other, step) for step in (1, 2, 3))

    def gather_ring():
        arrive(gather)
        for colour, axis in enumerate(first_axis):
            here = s_buf.at[colour, place[axis]]
            ring.extend((links.copy(here, here, axis, 1), links.copy(here, here, axis, -1)))

    def gather_relay():
        arrive(ring)
        for colour, axis in enumerate(first_axis):
            low = s_buf.at[colour, place.of(axis, -1), pl.ds(0, 2)]
            high = s_buf.at[colour, place.of(axis, 1), pl.ds(2, 2)]
            relay.extend((links.copy(low, low, axis, 1), links.copy(high, high, axis, -1)))

    def trade(step, moment):
        to = lax.rem(me + step, 32)
        col = pl.ds(pl.multiple_of(lax.rem(to, tiles) * 128, 128), 128)
        return pltpu.make_async_remote_copy(
            src_ref=(m1_ref, m2_ref)[moment].at[:, col],
            dst_ref=mc_buf.at[moment, me],
            send_sem=msend.at[moment, step],
            recv_sem=mrecv.at[moment, step],
            device_id=device({**place.at, **plane_place(to)}),
            device_id_type=MESH,
        ), to

    def trade_start(step, carry):
        for moment in range(2):
            out, to = trade(step, moment)
            pl.when(to < tiles)(functools.partial(begin, out))
        return carry

    def trade_end(step, carry):
        for moment in range(2):
            out, to = trade(step, moment)
            pl.when(to < tiles)(functools.partial(sent, out))
            pl.when(me < tiles)(functools.partial(came, out))
        return carry

    own_col = pl.ds(pl.multiple_of(lax.rem(me, tiles) * 128, 128), 128)
    gather_first()
    lax.fori_loop(1, 32, trade_start, 0)
    mc_buf[0, me] = m1_ref[:, own_col]
    mc_buf[1, me] = m2_ref[:, own_col]
    grams.end()

    size = 128
    rank = z_buf.shape[0]
    for p in range(rank // size):
        z_buf[:, p * size : p * size + size] = totals[0, p // 2, p % 2].reshape(rank, size)

    mix = mixes.steps()

    def both(*jobs):
        def run():
            for job in jobs:
                job()

        return run

    inverse_factor(
        z_buf,
        ticks=(
            both(mix[1]),
            both(gather_ring),
            both(mix[2]),
            both(mix[3], gather_relay),
            both(mix[4]),
            both(mix[5]),
            both(mix[6]),
            both(mix[7]),
        ),
    )
    arrive(relay)

    blocks = x_buf.shape[0]
    stack = [
        s_buf[colour, place.of(first_axis[colour], steps[i])].reshape(rows, rank) for i in range(4) for colour in range(2)
    ]
    whole = jnp.concatenate(stack, axis=0)
    middle = rank // 2
    dims = (((1,), (1,)), ((), ()))
    for start in (0, middle):
        deep_end = start + middle
        b_low[start:deep_end] = lax.dot_general(
            z_buf[start:deep_end, 0:deep_end], whole[:, 0:deep_end], dims, precision=HI, preferred_element_type=f32
        ).astype(bf16)

    width = x_buf.shape[-1]
    cut = width // 2
    axes = (("y", "z"), ("z", "y"))
    across, firsts, fulls, lasts = {}, {}, {}, {}

    def multiply(b):
        block = g_buf[:, :, :, b * width : b * width + width].reshape(8 * rows, width)
        out = jnp.dot(b_low[...], block, preferred_element_type=f32)
        x_buf[b] = out.reshape(x_buf.shape[1:])
        across[b] = links.copy(x_buf.at[b, :, :, 1 - c], x_in.at[b], "c", 1)

    def start_ring(b):
        across[b].wait_recv()
        total = x_buf[b, :, :, c] + x_in[b]
        y_buf[b, 0] = total[..., :cut]
        for i in range(SIDE):
            y_buf[b, 1, :, i] = total[i, :, :, cut:]
        for colour in range(2):
            axis = axes[colour][0]
            far = place.of(axis, 2)
            firsts[b, colour] = (
                links.copy(y_buf.at[b, colour, far, pl.ds(0, 2)], r_half.at[b, colour, 0], axis, 1),
                links.copy(y_buf.at[b, colour, far, pl.ds(2, 2)], r_half.at[b, colour, 1], axis, -1),
            )

    def pass_on(b):
        for colour in range(2):
            axis = axes[colour][0]
            outs = []
            for side in range(2):
                firsts[b, colour][side].wait_recv()
                to = place.of(axis, (1, -1)[side])
                y_buf[b, colour, to, 2 * side : 2 * side + 2] += r_half[b, colour, side]
                outs.append(links.copy(y_buf.at[b, colour, to], r_full.at[b, colour, side], axis, (1, -1)[side]))
            fulls[b, colour] = outs

    def second_axis(b):
        for colour in range(2):
            axis, other = axes[colour]
            arrive(fulls[b, colour])
            p_buf[b, colour] = y_buf[b, colour, place[axis]] + (r_full[b, colour, 0] + r_full[b, colour, 1])
            lasts[b, colour] = [
                links.copy(p_buf.at[b, colour, place.of(other, step)], p_in.at[b, colour, step - 1], other, step)
                for step in (1, 2, 3)
            ]

    def complete(b):
        for colour in range(2):
            arrive(lasts[b, colour])
            start = b * width + colour * cut
            pa_ref[:, start : start + cut] = p_buf[b, colour, place[axes[colour][1]]] + p_in[b, colour, 1]
            pb_ref[:, start : start + cut] = p_in[b, colour, 0] + p_in[b, colour, 2]

    def give(step):
        to, source = lax.rem(me + step, 32), lax.rem(me + (32 - step), 32)
        return pltpu.make_async_remote_copy(
            src_ref=turned.at[:, to],
            dst_ref=tin_ref.at[:, :, own_col],
            send_sem=tsend.at[step],
            recv_sem=trecv.at[step],
            device_id=device({**place.at, **plane_place(to)}),
            device_id_type=MESH,
        ), source

    def give_start(step, carry):
        out, source = give(step)
        pl.when(me < tiles)(functools.partial(begin, out))
        return carry

    def give_end(step, carry):
        out, source = give(step)
        pl.when(me < tiles)(functools.partial(sent, out))
        pl.when(source < tiles)(functools.partial(came, out))
        return carry

    def turn():
        lax.fori_loop(1, 32, trade_end, 0)
        mixed = jnp.concatenate([totals[1, p // 2, p % 2].reshape(rank, size) for p in range(rank // size)], axis=1)
        corr = jnp.dot(z_buf[...], mixed, precision=HI, preferred_element_type=f32)
        shape = turned.shape[1:]
        old = mc_buf[0].reshape(rank, size)
        turned[0] = jnp.dot(corr, old, precision=HI, preferred_element_type=f32).reshape(shape)
        old = mc_buf[1].reshape(rank, size)
        turned[1] = jnp.dot(corr * corr, old, precision=HI, preferred_element_type=f32).reshape(shape)
        lax.fori_loop(1, 32, give_start, 0)

        @pl.when(me < tiles)
        def _():
            tin_ref[:, :, own_col] = turned[:, me]

    jobs = tuple(zip((start_ring, pass_on, second_axis, complete), LAGS))
    for tick in range(blocks + LAGS[-1]):
        if tick < blocks:
            multiply(tick)
        for job, lag in reversed(jobs):
            if 0 <= tick - lag < blocks:
                job(tick - lag)
        if tick == TURN:
            turn()
    lax.fori_loop(1, 32, give_end, 0)
    links.finish()


def call(grad, test, old, first, second):
    rows, cols = grad.shape
    rank = test.shape[1]
    deep = 512
    block, small = rows // 8, rows // 32
    strip = rank // SIDE
    bit = strip // SIDE
    own_rank, tiles = first.shape[0], cols // 128
    width = 512
    blocks = cols // width
    cut = width // 2
    buf = lambda *shape: pltpu.VMEM(shape, f32)
    dma = lambda *shape: pltpu.SemaphoreType.DMA(shape)
    copies = 24 + 2 * 40 + 16 + 15 * blocks
    out = jax.ShapeDtypeStruct((own_rank, cols), f32)
    return pl.pallas_call(
        functools.partial(kernel, tiles),
        out_shape=(out, out, jax.ShapeDtypeStruct((2, own_rank, cols), f32)),
        in_specs=[ANY, ANY, ANY, VMEM, VMEM],
        out_specs=(VMEM, VMEM, VMEM),
        scratch_shapes=[
            pltpu.VMEM((4, 2, block, cols), bf16),
            pltpu.VMEM((cols // deep, deep, rank), jnp.int32),
            pltpu.VMEM((cols // deep, deep, rank), bf16),
            buf(4, 2, block, rank),
            buf(2, 2, block // 2, rank),
            buf(2, 2, block, rank),
            buf(2, SIDE, small, rank),
            buf(2, 3, small, rank),
            buf(2, small, rank),
            buf(2, small, rank),
            buf(2, 2, 2, SIDE, strip, 128),
            buf(2, 2, SIDE, strip, 128),
            buf(2, 2, SIDE, strip, 128),
            buf(2, 2, 3, strip, 128),
            buf(2, 2, SIDE, bit, 128),
            buf(2, 2, 3, bit, 128),
            buf(2, 2, bit, 128),
            buf(2, 2, 3, bit, 128),
            buf(2, 2, bit, 128),
            buf(2, 2, SIDE, bit, 128),
            buf(2, 2, SIDE, SIDE, bit, 128),
            buf(2, 2, 2, SIDE, SIDE, bit, 128),
            buf(2, SIDE, SIDE, small, rank),
            buf(2, 32, own_rank, 128),
            buf(rank, rank),
            buf(2, 32, own_rank, 128),
            pltpu.VMEM((rank, rows), bf16),
            buf(blocks, SIDE, SIDE, 2, own_rank, width),
            buf(blocks, SIDE, SIDE, own_rank, width),
            buf(blocks, 2, SIDE, SIDE, own_rank, cut),
            buf(blocks, 2, 2, 2, own_rank, cut),
            buf(blocks, 2, 2, SIDE, own_rank, cut),
            buf(blocks, 2, SIDE, own_rank, cut),
            buf(blocks, 2, 3, own_rank, cut),
            dma(copies),
            dma(copies),
            dma(2, 32),
            dma(2, 32),
            dma(32),
            dma(32),
            dma(32),
        ],
        compiler_params=pltpu.CompilerParams(
            collective_id=0, has_side_effects=True, vmem_limit_bytes=67043328
        ),
    )(
        grad.reshape(2, SIDE, block, cols),
        test.reshape(cols // deep, deep, rank),
        old.reshape(2, SIDE, SIDE, small, rank),
        first,
        second,
    )


def local(gradients, test_matrix, old_basis, first_moment, second_moment):
    one, other, turned = call(gradients[0], test_matrix, old_basis, first_moment, second_moment)
    projected = one + other
    first_new = 0.9 * turned[0] + 0.1 * projected
    second_new = 0.95 * turned[1] + 0.05 * projected * projected
    return projected, first_new, second_new


def solution(mesh):
    moment = P(("dp", "row"), "col")
    in_specs = (P("dp", "row", "col"), P("col", None), P("row", None), moment, moment)
    return jax.shard_map(local, mesh=mesh, in_specs=in_specs, out_specs=(moment,) * 3, check_vma=False)
```

time: 434 us -> 138 us (0.32)
  waiting for transfers between devices: 343 us -> 0 us
  Pallas kernels: 23.3 us -> 134 us
  matrix products: 48.8 us -> 0 us
  between operations: 13.8 us -> 0.64 us
    psum x2 -> x0, waiting for transfers between devices: 159 us -> none  [the longest x1 93.5 us: local(): sketch = lax.psum(partial_value, ('dp', 'col'))]
    pallas_call x1, Pallas kernels: 23.3 us -> 134 us  [call(): pl.pallas_call(functools.partial(kernel, tiles), out_shape=(out, out, jax...]
    all_gather x2 -> x0, waiting for transfers between devices: 97.9 us -> none  [the longest x1 52.3 us: local(): lax.all_gather(second_moment, ('dp', 'row'), axis=0, tiled=True)]
    reduce_scatter x1 -> x0, waiting for transfers between devices: 85.3 us -> none  [local(): lax.psum_scatter(lax.dot_general(basis_low, replica_grad, (((0,), (0,)),...]
    dot_general x7 -> x0, matrix products: 48.8 us -> none  [the longest x1 10.6 us: local(): jnp.dot(replica_grad, test_values, preferred_element_type=f32)]
  transfers between devices with their start and end apart: 5 -> 0, of which waited for: 5 -> 0; matrix products, arithmetic and copies ran while one was open for 2% -> 0% of each run, Pallas kernels for 0% -> 0%
where the time goes in v3:
time: 138 us
  Pallas kernels  134 us (97%)
  other arithmetic  3.65 us (3%)
    pallas_call x1, Pallas kernels, call(): pl.pallas_call(functools.partial(kernel, tiles), out_shape=(out, out, jax...  134 us

profile of v3, /device:TPU:0, one launch (start us, length us, event | category | flops | bytes accessed | tf_op | source)
XLA Modules:
  0.0 138.2 jit_solution(7046801341440776003)
XLA Ops:
  0.6 133.9 %shard_map.76 = (f32[16,3584]{1,0:T(8,128)}, f32[16,3584]{1,0:T(8,128)}, f32[2,16,3584]{2,1,0:T(8,128)}) custom-call(bf16[2,4,128,3584]{3,2,1,0:T(8,128)(2,1)} %bitcast.7, s32[7,512,512]{2,1,0:T(8,128)} %bitcast.8, f32[2,4,4,32,512]{4,3,2,1,0:T(8,128)} %bitcast.9, f32[16,3584]{1,0:T(8,128)} %m1_ref.1, f32[16,3584]{1,0:T(8,128)} %m2_ref.1), custom_call_target="tpu_custom_call" | custom-call | tf_op jit(solution)/shard_map/pallas_call | solution.py:620
  134.5 1.9 %fusion = (f32[16,3584]{1,0:T(8,128)}, f32[16,3584]{1,0:T(8,128)S(1)}) fusion(f32[2,16,3584]{2,1,0:T(8,128)} %get-tuple-element.8, f32[16,3584]{1,0:T(8,128)} %get-tuple-element.6, f32[16,3584]{1,0:T(8,128)} %get-tuple-element.7), kind=kLoop, calls=%fused_computation.1 | loop fusion | flops 286720 | bytes 1146880 | tf_op jit(solution)/shard_map/add | solution.py:684
  136.4 0.0 copy-start
  136.5 1.8 %bitcast_add_fusion = f32[16,3584]{1,0:T(8,128)} fusion(f32[16,3584]{1,0:T(8,128)S(1)} %get-tuple-element.10, f32[2,16,3584]{2,1,0:T(8,128)} %get-tuple-element.8), kind=kLoop, calls=%fused_computation.2 | loop fusion | flops 172032 | bytes 688128 | tf_op jit(solution)/shard_map/add | solution.py:683
  138.2 0.0 copy-done
Async XLA Ops:
  136.4 1.8 %copy-start = (f32[16,3584]{1,0:T(8,128)}, f32[16,3584]{1,0:T(8,128)S(1)}, u32[]{:S(2)}) copy-start(f32[16,3584]{1,0:T(8,128)S(1)} %get-tuple-element.10) | copy-start | bytes 688132

commit v4 on v3

--- a/solution.py
+++ b/solution.py
@@ -9,7 +9,7 @@
 f32 = jnp.float32
 
 
-def factor_diag(block, group):
+def factor_diag(block, group, middle=None):
     size = block.shape[0]
     tiles = size // 8
     z = [block[8 * b : 8 * b + 8, :] for b in range(tiles)]
@@ -17,6 +17,8 @@
     sub = lax.broadcasted_iota(jnp.int32, (8, size), 0)
     full = lambda v: jnp.broadcast_to(v, (8, size))
     for b in range(tiles):
+        if b == tiles // 2 and middle is not None:
+            middle()
         pivots = jnp.ones((8, size), f32)
         for r in range(0, 8, group):
             j = 8 * b + r
@@ -32,7 +34,7 @@
                 for u in range(t + 1, group):
                     m = piv[t][u] * inv[t]
                     for s in range(u, group):
-                        piv[u][s] = piv[u][s] - m * piv[t][s]
+                        piv[u][s] = piv[u][s] - piv[t][u] * piv[t][s] * inv[t]
                     rows[u] = rows[u] - m * rows[t]
             for i in range(b, tiles):
                 cols = [full_col(z[i], j + t, size) for t in range(group)]
@@ -61,11 +63,9 @@
     blocks = n // size
     for k in range(blocks):
         at = slice(k * size, k * size + size)
-        inv = factor_diag(z[at, at], group)
+        inv = factor_diag(z[at, at], group, ticks[2 * k] if ticks else None)
         z[at, :] = jnp.dot(inv, z[at, :], precision=HI, preferred_element_type=f32)
         z[at, at] = inv
-        if 2 * k < len(ticks):
-            ticks[2 * k]()
         if k + 1 < blocks:
             below = slice(k * size + size, n)
             low = z[at, below]
@@ -83,8 +83,6 @@
 SIDE = 4
 VMEM = pl.BlockSpec(memory_space=pltpu.VMEM)
 ANY = pl.BlockSpec(memory_space=pl.ANY)
-LAGS = (1, 3, 5, 7)
-TURN = 3
 
 
 def plane_place(p):
@@ -184,7 +182,7 @@
 
 
 class Total:
-    orders = (("x", "y", "z"), ("y", "z", "x"))
+    orders = (("x", "z", "y"), ("y", "z", "x"))
 
     def __init__(self, place, links, parts, core_in, v0, r1, v1, r2, v2, r3, v3, w1, w0, out):
         self.place, self.links, self.parts, self.core_in, self.out = place, links, parts, core_in, out
@@ -269,10 +267,10 @@
 
 
 def kernel(
-    tiles, g_hbm, t_hbm, o_hbm, m1_ref, m2_ref, pa_ref, pb_ref, tin_ref,
+    tiles, g_hbm, t_hbm, o_hbm, m1_ref, m2_ref, pin_ref, tin_ref,
     g_buf, t_buf, t_low, part, half, full, quarter, second, own, o_buf,
     parts, core_in, v0, r1, v1, r2, v2, r3, v3, w1, w0, totals,
-    s_buf, mc_buf, z_buf, turned, b_low,
+    s_buf, m_buf, mc_buf, z_buf, corr_buf, turned, made, st_buf,
     x_buf, x_in, y_buf, r_half, r_full, p_buf, p_in,
     send, recv, msend, mrecv, tsend, trecv, local_sem,
 ):
@@ -288,10 +286,6 @@
         pl.semaphore_signal(barrier, inc=1, device_id=device(to), device_id_type=MESH)
         return carry
 
-    for step in (1, 2, 3):
-        pl.semaphore_signal(barrier, inc=1, device_id=place.devices["x", step], device_id_type=MESH)
-    lax.fori_loop(1, 32, greet, 0)
-
     loads = []
 
     def load(src, dst):
@@ -316,6 +310,10 @@
     for i in (1, 2, 3):
         load_g(i)
     o_loads = [load(o_hbm.at[0, x, y], o_buf.at[0]), load(o_hbm.at[1, y, x], o_buf.at[1])]
+
+    for step in (1, 2, 3):
+        pl.semaphore_signal(barrier, inc=1, device_id=place.devices["x", step], device_id_type=MESH)
+    lax.fori_loop(1, 32, greet, 0)
 
     def product(i, k):
         lhs = g_buf[i, :, :, pl.ds(pl.multiple_of(k * deep, deep), deep)].reshape(2 * rows, deep)
@@ -338,7 +336,34 @@
 
             lax.fori_loop(1, chunks, more, 0)
 
+    def trade(step):
+        to = lax.rem(me + step, 32)
+        col = pl.ds(pl.multiple_of(lax.rem(to, tiles) * 128, 128), 128)
+        return pltpu.make_async_remote_copy(
+            src_ref=m_buf.at[:, :, col],
+            dst_ref=mc_buf.at[:, me],
+            send_sem=msend.at[step],
+            recv_sem=mrecv.at[step],
+            device_id=device({**place.at, **plane_place(to)}),
+            device_id_type=MESH,
+        ), to
+
+    def trade_start(step, carry):
+        out, to = trade(step)
+        pl.when(to < tiles)(functools.partial(begin, out))
+        return carry
+
+    def trade_end(step, carry):
+        out, to = trade(step)
+        pl.when(to < tiles)(functools.partial(sent, out))
+        pl.when(me < tiles)(functools.partial(came, out))
+        return carry
+
+    own_col = pl.ds(pl.multiple_of(lax.rem(me, tiles) * 128, 128), 128)
+
     matmul(0)
+    m_buf[0] = m1_ref[...]
+    m_buf[1] = m2_ref[...]
     pl.semaphore_wait(barrier, 34)
     mid = rows // 2
     up, down, ups, downs, later = [], [], [], [], []
@@ -346,19 +371,23 @@
         up.append(links.copy(part.at[0, colour, pl.ds(0, mid)], half.at[0, colour], axis, 1))
         down.append(links.copy(part.at[0, colour, pl.ds(mid, mid)], half.at[1, colour], axis, -1))
     matmul(1)
+    low, high = pl.ds(0, mid), pl.ds(mid, mid)
+    for colour, axis in enumerate(first_axis):
+        ups.append(links.copy(part.at[1, colour, high], full.at[0, colour, high], axis, 1))
+    matmul(2)
+    for colour, axis in enumerate(first_axis):
+        downs.append(links.copy(part.at[2, colour, low], full.at[1, colour, low], axis, -1))
     for colour, axis in enumerate(first_axis):
         up[colour].wait_recv()
-        part[1, colour, 0:mid] += half[0, colour]
-        ups.append(links.copy(part.at[1, colour], full.at[0, colour], axis, 1))
-    matmul(2)
-    for colour, axis in enumerate(first_axis):
+        part[1, colour, low] += half[0, colour]
+        ups.append(links.copy(part.at[1, colour, low], full.at[0, colour, low], axis, 1))
         down[colour].wait_recv()
-        part[2, colour, mid:] += half[1, colour]
-        downs.append(links.copy(part.at[2, colour], full.at[1, colour], axis, -1))
+        part[2, colour, high] += half[1, colour]
+        downs.append(links.copy(part.at[2, colour, high], full.at[1, colour, high], axis, -1))
     matmul(3)
     for colour, axis in enumerate(first_axis):
         other = first_axis[1 - colour]
-        arrive((ups[colour], downs[colour]))
+        arrive((ups[colour], downs[colour], ups[2 + colour], downs[2 + colour]))
         total = part[3, colour] + (full[0, colour] + full[1, colour])
         quarter[colour] = total.reshape(quarter.shape[1:])
         later.append(
@@ -390,214 +419,198 @@
         )
         for kind in range(2)
     )
+    gather, ring, relay = [], [], []
+
+    def gather_first():
+        for colour in range(2):
+            axis, other = first_axis[colour], first_axis[1 - colour]
+            s_buf[colour, place[axis], place[other]] = own[colour]
+            here = s_buf.at[colour, place[axis], place[other]]
+            gather.extend(links.copy(own.at[colour], here, other, step) for step in (1, 2, 3))
+
+    def gather_ring():
+        arrive(gather)
+        for colour, axis in enumerate(first_axis):
+            here = s_buf.at[colour, place[axis]]
+            ring.extend((links.copy(here, here, axis, 1), links.copy(here, here, axis, -1)))
+
+    def gather_relay():
+        arrive(ring)
+        for colour, axis in enumerate(first_axis):
+            below = s_buf.at[colour, place.of(axis, -1), pl.ds(0, 2)]
+            above = s_buf.at[colour, place.of(axis, 1), pl.ds(2, 2)]
+            relay.extend((links.copy(below, below, axis, 1), links.copy(above, above, axis, -1)))
+
+    size = 128
+    rank = z_buf.shape[0]
+    axes = (("y", "z"), ("z", "y"))
+    across, firsts, fulls, lasts = [], [], [], []
+
+    def turn_sketch():
+        arrive(relay)
+        for i in range(4):
+            for colour in range(2):
+                value = s_buf[colour, place.of(first_axis[colour], steps[i])].reshape(rows, rank).T
+                start = (2 * i + colour) * rows
+                high = value.astype(bf16)
+                st_buf[0, :, start : start + rows] = high
+                st_buf[1, :, start : start + rows] = (value - high.astype(f32)).astype(bf16)
+
+    def multiply(b):
+        block = g_buf[:, :, :, b * deep : b * deep + deep].reshape(8 * rows, deep)
+        out = jnp.dot(st_buf[0], block, preferred_element_type=f32)
+        out += jnp.dot(st_buf[1], block, preferred_element_type=f32)
+        for i in range(deep // size):
+            p = b * (deep // size) + i
+            x_buf[p // 8, (p // 2) % 4, p % 2] = out[:, i * size : i * size + size].reshape(x_buf.shape[3:])
+        if b == chunks - 1:
+            for p in range(tiles, 32):
+                x_buf[p // 8, (p // 2) % 4, p % 2] = jnp.zeros(x_buf.shape[3:], f32)
+        for group in range(SIDE):
+            if b == min(2 * group + 1, chunks - 1):
+                across.append(links.copy(x_buf.at[group, :, 1 - c], x_in.at[group], "c", 1))
+
+    def reduce_core(i):
+        across[i].wait_recv()
+        total = x_buf[i, :, c] + x_in[i]
+        y_buf[0, i] = total[:, 0]
+        y_buf[1, :, i] = total[:, 1]
+
+    def reduce_ring():
+        for colour in range(2):
+            axis = axes[colour][0]
+            far = place.of(axis, 2)
+            firsts.append(links.copy(y_buf.at[colour, far, pl.ds(0, 2)], r_half.at[colour, 0], axis, 1))
+            firsts.append(links.copy(y_buf.at[colour, far, pl.ds(2, 2)], r_half.at[colour, 1], axis, -1))
+
+    def reduce_pass():
+        for colour in range(2):
+            axis = axes[colour][0]
+            for side in range(2):
+                firsts[2 * colour + side].wait_recv()
+                to = place.of(axis, (1, -1)[side])
+                y_buf[colour, to, 2 * side : 2 * side + 2] += r_half[colour, side]
+                fulls.append(links.copy(y_buf.at[colour, to], r_full.at[colour, side], axis, (1, -1)[side]))
+
+    def reduce_second():
+        arrive(fulls)
+        for colour in range(2):
+            axis, other = axes[colour]
+            p_buf[colour] = y_buf[colour, place[axis]] + (r_full[colour, 0] + r_full[colour, 1])
+            lasts.extend(
+                links.copy(p_buf.at[colour, place.of(other, step)], p_in.at[colour, step - 1], other, step)
+                for step in (1, 2, 3)
+            )
+
+    def reduced():
+        arrive(lasts)
+        return jnp.concatenate(
+            [tree(p_buf[colour, place[axes[colour][1]]], p_in[colour]) for colour in range(2)], axis=0
+        )
+
     share(mine, 0)
     grams.core()
+    gather_first()
     for out in o_loads:
         out.wait()
     share(o_buf[...].reshape(-1, wide), 1)
     grams.first()
     mixes.core()
+    gather_ring()
     grams.second()
     grams.third()
+    gather_relay()
     grams.back2()
     grams.back1()
+    lax.fori_loop(1, 32, trade_start, 0)
+    mc_buf[:, me] = m_buf[:, :, own_col]
+    turn_sketch()
+    multiply(0)
     grams.join()
-
-    gather, ring, relay = [], [], []
-
-    def gather_first():
-        for colour in range(2):
-            axis, other = first_axis[colour], first_axis[1 - colour]
-            s_buf[colour, place[axis], place[other]] = own[colour]
-            here = s_buf.at[colour, place[axis], place[other]]
-            gather.extend(links.copy(own.at[colour], here, other, step) for step in (1, 2, 3))
-
-    def gather_ring():
-        arrive(gather)
-        for colour, axis in enumerate(first_axis):
-            here = s_buf.at[colour, place[axis]]
-            ring.extend((links.copy(here, here, axis, 1), links.copy(here, here, axis, -1)))
-
-    def gather_relay():
-        arrive(ring)
-        for colour, axis in enumerate(first_axis):
-            low = s_buf.at[colour, place.of(axis, -1), pl.ds(0, 2)]
-            high = s_buf.at[colour, place.of(axis, 1), pl.ds(2, 2)]
-            relay.extend((links.copy(low, low, axis, 1), links.copy(high, high, axis, -1)))
-
-    def trade(step, moment):
-        to = lax.rem(me + step, 32)
-        col = pl.ds(pl.multiple_of(lax.rem(to, tiles) * 128, 128), 128)
-        return pltpu.make_async_remote_copy(
-            src_ref=(m1_ref, m2_ref)[moment].at[:, col],
-            dst_ref=mc_buf.at[moment, me],
-            send_sem=msend.at[moment, step],
-            recv_sem=mrecv.at[moment, step],
-            device_id=device({**place.at, **plane_place(to)}),
-            device_id_type=MESH,
-        ), to
-
-    def trade_start(step, carry):
-        for moment in range(2):
-            out, to = trade(step, moment)
-            pl.when(to < tiles)(functools.partial(begin, out))
-        return carry
-
-    def trade_end(step, carry):
-        for moment in range(2):
-            out, to = trade(step, moment)
-            pl.when(to < tiles)(functools.partial(sent, out))
-            pl.when(me < tiles)(functools.partial(came, out))
-        return carry
-
-    own_col = pl.ds(pl.multiple_of(lax.rem(me, tiles) * 128, 128), 128)
-    gather_first()
-    lax.fori_loop(1, 32, trade_start, 0)
-    mc_buf[0, me] = m1_ref[:, own_col]
-    mc_buf[1, me] = m2_ref[:, own_col]
+    mixes.first()
+    multiply(1)
+    multiply(2)
+    multiply(3)
     grams.end()
-
-    size = 128
-    rank = z_buf.shape[0]
+    mixes.second()
+    multiply(4)
+    multiply(5)
+    mixes.third()
+    multiply(6)
+
     for p in range(rank // size):
         z_buf[:, p * size : p * size + size] = totals[0, p // 2, p % 2].reshape(rank, size)
 
-    mix = mixes.steps()
-
-    def both(*jobs):
-        def run():
-            for job in jobs:
-                job()
-
-        return run
+    def early():
+        mixes.back2()
+        for i in range(SIDE - 1):
+            reduce_core(i)
+
+    def start():
+        mixes.back1()
+        reduce_core(SIDE - 1)
+        reduce_ring()
+
+    def nothing():
+        pass
 
     inverse_factor(
         z_buf,
-        ticks=(
-            both(mix[1]),
-            both(gather_ring),
-            both(mix[2]),
-            both(mix[3], gather_relay),
-            both(mix[4]),
-            both(mix[5]),
-            both(mix[6]),
-            both(mix[7]),
-        ),
+        ticks=(early, start, nothing, mixes.join, reduce_pass, mixes.end, nothing, nothing),
     )
-    arrive(relay)
-
-    blocks = x_buf.shape[0]
-    stack = [
-        s_buf[colour, place.of(first_axis[colour], steps[i])].reshape(rows, rank) for i in range(4) for colour in range(2)
-    ]
-    whole = jnp.concatenate(stack, axis=0)
-    middle = rank // 2
-    dims = (((1,), (1,)), ((), ()))
-    for start in (0, middle):
-        deep_end = start + middle
-        b_low[start:deep_end] = lax.dot_general(
-            z_buf[start:deep_end, 0:deep_end], whole[:, 0:deep_end], dims, precision=HI, preferred_element_type=f32
-        ).astype(bf16)
-
-    width = x_buf.shape[-1]
-    cut = width // 2
-    axes = (("y", "z"), ("z", "y"))
-    across, firsts, fulls, lasts = {}, {}, {}, {}
-
-    def multiply(b):
-        block = g_buf[:, :, :, b * width : b * width + width].reshape(8 * rows, width)
-        out = jnp.dot(b_low[...], block, preferred_element_type=f32)
-        x_buf[b] = out.reshape(x_buf.shape[1:])
-        across[b] = links.copy(x_buf.at[b, :, :, 1 - c], x_in.at[b], "c", 1)
-
-    def start_ring(b):
-        across[b].wait_recv()
-        total = x_buf[b, :, :, c] + x_in[b]
-        y_buf[b, 0] = total[..., :cut]
-        for i in range(SIDE):
-            y_buf[b, 1, :, i] = total[i, :, :, cut:]
-        for colour in range(2):
-            axis = axes[colour][0]
-            far = place.of(axis, 2)
-            firsts[b, colour] = (
-                links.copy(y_buf.at[b, colour, far, pl.ds(0, 2)], r_half.at[b, colour, 0], axis, 1),
-                links.copy(y_buf.at[b, colour, far, pl.ds(2, 2)], r_half.at[b, colour, 1], axis, -1),
-            )
-
-    def pass_on(b):
-        for colour in range(2):
-            axis = axes[colour][0]
-            outs = []
-            for side in range(2):
-                firsts[b, colour][side].wait_recv()
-                to = place.of(axis, (1, -1)[side])
-                y_buf[b, colour, to, 2 * side : 2 * side + 2] += r_half[b, colour, side]
-                outs.append(links.copy(y_buf.at[b, colour, to], r_full.at[b, colour, side], axis, (1, -1)[side]))
-            fulls[b, colour] = outs
-
-    def second_axis(b):
-        for colour in range(2):
-            axis, other = axes[colour]
-            arrive(fulls[b, colour])
-            p_buf[b, colour] = y_buf[b, colour, place[axis]] + (r_full[b, colour, 0] + r_full[b, colour, 1])
-            lasts[b, colour] = [
-                links.copy(p_buf.at[b, colour, place.of(other, step)], p_in.at[b, colour, step - 1], other, step)
-                for step in (1, 2, 3)
-            ]
-
-    def complete(b):
-        for colour in range(2):
-            arrive(lasts[b, colour])
-            start = b * width + colour * cut
-            pa_ref[:, start : start + cut] = p_buf[b, colour, place[axes[colour][1]]] + p_in[b, colour, 1]
-            pb_ref[:, start : start + cut] = p_in[b, colour, 0] + p_in[b, colour, 2]
-
-    def give(step):
+
+    def give(step, value, into, sems):
         to, source = lax.rem(me + step, 32), lax.rem(me + (32 - step), 32)
         return pltpu.make_async_remote_copy(
-            src_ref=turned.at[:, to],
-            dst_ref=tin_ref.at[:, :, own_col],
-            send_sem=tsend.at[step],
-            recv_sem=trecv.at[step],
+            src_ref=value.at[:, to],
+            dst_ref=into.at[:, :, own_col],
+            send_sem=tsend.at[sems, step],
+            recv_sem=trecv.at[sems, step],
             device_id=device({**place.at, **plane_place(to)}),
             device_id_type=MESH,
         ), source
 
-    def give_start(step, carry):
-        out, source = give(step)
-        pl.when(me < tiles)(functools.partial(begin, out))
+    gifts = ((turned, tin_ref), (made, pin_ref))
+
+    def give_start(sems):
+        def one(step, carry):
+            out, source = give(step, *gifts[sems], sems)
+            pl.when(me < tiles)(functools.partial(begin, out))
+            return carry
+
+        lax.fori_loop(1, 32, one, 0)
+
+    def give_end(step, carry):
+        for sems in range(2):
+            out, source = give(step, *gifts[sems], sems)
+            pl.when(me < tiles)(functools.partial(sent, out))
+            pl.when(source < tiles)(functools.partial(came, out))
         return carry
 
-    def give_end(step, carry):
-        out, source = give(step)
-        pl.when(me < tiles)(functools.partial(sent, out))
-        pl.when(source < tiles)(functools.partial(came, out))
-        return carry
-
-    def turn():
-        lax.fori_loop(1, 32, trade_end, 0)
-        mixed = jnp.concatenate([totals[1, p // 2, p % 2].reshape(rank, size) for p in range(rank // size)], axis=1)
-        corr = jnp.dot(z_buf[...], mixed, precision=HI, preferred_element_type=f32)
-        shape = turned.shape[1:]
-        old = mc_buf[0].reshape(rank, size)
-        turned[0] = jnp.dot(corr, old, precision=HI, preferred_element_type=f32).reshape(shape)
-        old = mc_buf[1].reshape(rank, size)
-        turned[1] = jnp.dot(corr * corr, old, precision=HI, preferred_element_type=f32).reshape(shape)
-        lax.fori_loop(1, 32, give_start, 0)
-
-        @pl.when(me < tiles)
-        def _():
-            tin_ref[:, :, own_col] = turned[:, me]
-
-    jobs = tuple(zip((start_ring, pass_on, second_axis, complete), LAGS))
-    for tick in range(blocks + LAGS[-1]):
-        if tick < blocks:
-            multiply(tick)
-        for job, lag in reversed(jobs):
-            if 0 <= tick - lag < blocks:
-                job(tick - lag)
-        if tick == TURN:
-            turn()
+    mixed = jnp.concatenate([totals[1, p // 2, p % 2].reshape(rank, size) for p in range(rank // size)], axis=1)
+    half_rank = rank // 2
+    for start_row in (0, half_rank):
+        end_row = start_row + half_rank
+        corr_buf[start_row:end_row] = jnp.dot(
+            z_buf[start_row:end_row, 0:end_row], mixed[0:end_row], precision=HI, preferred_element_type=f32
+        )
+    reduce_second()
+    lax.fori_loop(1, 32, trade_end, 0)
+    corr = corr_buf[...]
+    shape = turned.shape[1:]
+    old = mc_buf[0].reshape(rank, size)
+    turned[0] = jnp.dot(corr, old, precision=HI, preferred_element_type=f32).reshape(shape)
+    old = mc_buf[1].reshape(rank, size)
+    turned[1] = jnp.dot(corr * corr, old, precision=HI, preferred_element_type=f32).reshape(shape)
+    give_start(0)
+    made[0] = jnp.dot(z_buf[...], reduced(), precision=HI, preferred_element_type=f32).reshape(shape)
+    give_start(1)
+
+    @pl.when(me < tiles)
+    def _():
+        tin_ref[:, :, own_col] = turned[:, me]
+        pin_ref[:, :, own_col] = made[:, me]
+
     lax.fori_loop(1, 32, give_end, 0)
     links.finish()
 
@@ -610,18 +623,15 @@
     strip = rank // SIDE
     bit = strip // SIDE
     own_rank, tiles = first.shape[0], cols // 128
-    width = 512
-    blocks = cols // width
-    cut = width // 2
+    cut = rank // 2
     buf = lambda *shape: pltpu.VMEM(shape, f32)
     dma = lambda *shape: pltpu.SemaphoreType.DMA(shape)
-    copies = 24 + 2 * 40 + 16 + 15 * blocks
-    out = jax.ShapeDtypeStruct((own_rank, cols), f32)
+    copies = 32 + 2 * 40 + 40
     return pl.pallas_call(
         functools.partial(kernel, tiles),
-        out_shape=(out, out, jax.ShapeDtypeStruct((2, own_rank, cols), f32)),
+        out_shape=tuple(jax.ShapeDtypeStruct((n, own_rank, cols), f32) for n in (1, 2)),
         in_specs=[ANY, ANY, ANY, VMEM, VMEM],
-        out_specs=(VMEM, VMEM, VMEM),
+        out_specs=(VMEM, VMEM),
         scratch_shapes=[
             pltpu.VMEM((4, 2, block, cols), bf16),
             pltpu.VMEM((cols // deep, deep, rank), jnp.int32),
@@ -646,23 +656,26 @@
             buf(2, 2, SIDE, SIDE, bit, 128),
             buf(2, 2, 2, SIDE, SIDE, bit, 128),
             buf(2, SIDE, SIDE, small, rank),
+            buf(2, own_rank, cols),
             buf(2, 32, own_rank, 128),
             buf(rank, rank),
+            buf(rank, rank),
             buf(2, 32, own_rank, 128),
-            pltpu.VMEM((rank, rows), bf16),
-            buf(blocks, SIDE, SIDE, 2, own_rank, width),
-            buf(blocks, SIDE, SIDE, own_rank, width),
-            buf(blocks, 2, SIDE, SIDE, own_rank, cut),
-            buf(blocks, 2, 2, 2, own_rank, cut),
-            buf(blocks, 2, 2, SIDE, own_rank, cut),
-            buf(blocks, 2, SIDE, own_rank, cut),
-            buf(blocks, 2, 3, own_rank, cut),
+            buf(1, 32, own_rank, 128),
+            pltpu.VMEM((2, rank, rows), bf16),
+            buf(SIDE, SIDE, 2, 2, cut, 128),
+            buf(SIDE, SIDE, 2, cut, 128),
+            buf(2, SIDE, SIDE, cut, 128),
+            buf(2, 2, 2, cut, 128),
+            buf(2, 2, SIDE, cut, 128),
+            buf(2, SIDE, cut, 128),
+            buf(2, 3, cut, 128),
             dma(copies),
             dma(copies),
+            dma(32),
+            dma(32),
             dma(2, 32),
             dma(2, 32),
-            dma(32),
-            dma(32),
             dma(32),
         ],
         compiler_params=pltpu.CompilerParams(
@@ -677,12 +690,21 @@
     )
 
 
+def finish_kernel(made_ref, turned_ref, projected_ref, first_ref, second_ref):
+    projected = made_ref[0]
+    projected_ref[...] = projected
+    first_ref[...] = 0.9 * turned_ref[0] + 0.1 * projected
+    second_ref[...] = 0.95 * turned_ref[1] + 0.05 * projected * projected
+
+
 def local(gradients, test_matrix, old_basis, first_moment, second_moment):
-    one, other, turned = call(gradients[0], test_matrix, old_basis, first_moment, second_moment)
-    projected = one + other
-    first_new = 0.9 * turned[0] + 0.1 * projected
-    second_new = 0.95 * turned[1] + 0.05 * projected * projected
-    return projected, first_new, second_new
+    made, turned = call(gradients[0], test_matrix, old_basis, first_moment, second_moment)
+    return pl.pallas_call(
+        finish_kernel,
+        out_shape=(jax.ShapeDtypeStruct(made.shape[1:], f32),) * 3,
+        in_specs=[VMEM] * 2,
+        out_specs=(VMEM,) * 3,
+    )(made, turned)
 
 
 def solution(mesh):

time: 138 us -> 119 us (0.86); the launches traced: 138 us -> 118 us
  Pallas kernels: 134 us -> 117 us
  other arithmetic: 3.65 us -> 0 us
    pallas_call x1 -> x2, Pallas kernels: 134 us -> 117 us  [the longest x1 115 us: call(): pl.pallas_call(functools.partial(kernel, tiles), out_shape=tuple((jax.Sha...]
    add x2 -> x0, other arithmetic: 3.65 us -> none  [the longest x1 1.9 us: local(): second_new = 0.95 * turned[1] + 0.05 * projected * projected]
where the time goes in v4:
time: 119 us; the launch traced here: 118 us
  Pallas kernels  117 us (98%)
    pallas_call x1, Pallas kernels, call(): pl.pallas_call(functools.partial(kernel, tiles), out_shape=tuple((jax.Sha...  115 us

profile of v4, /device:TPU:0, one launch (start us, length us, event | category | flops | bytes accessed | tf_op | source)
XLA Modules:
  0.0 117.7 jit_solution(15037195262972921736)
XLA Ops:
  0.6 115.0 %shard_map.76 = (f32[1,16,3584]{2,1,0:T(8,128)}, f32[2,16,3584]{2,1,0:T(8,128)}) custom-call(bf16[2,4,128,3584]{3,2,1,0:T(8,128)(2,1)} %bitcast.3, s32[7,512,512]{2,1,0:T(8,128)} %bitcast.4, f32[2,4,4,32,512]{4,3,2,1,0:T(8,128)} %bitcast.5, f32[16,3584]{1,0:T(8,128)} %m1_ref.1, f32[16,3584]{1,0:T(8,128)} %m2_ref.1), custom_call_target="tpu_custom_call" | custom-call | tf_op jit(solution)/shard_map/pallas_call | solution.py:630
  115.7 2.0 %shard_map.77 = (f32[16,3584]{1,0:T(8,128)}, f32[16,3584]{1,0:T(8,128)}, f32[16,3584]{1,0:T(8,128)}) custom-call(f32[1,16,3584]{2,1,0:T(8,128)} %get-tuple-element.5.made_ref, f32[2,16,3584]{2,1,0:T(8,128)} %get-tuple-element.6.turned_ref), custom_call_target="tpu_custom_call" | custom-call | tf_op jit(solution)/shard_map/pallas_call | solution.py:702

commit v5 on v4

--- a/solution.py
+++ b/solution.py
@@ -9,7 +9,7 @@
 f32 = jnp.float32
 
 
-def factor_diag(block, group, middle=None):
+def factor_diag(block, group, hooks):
     size = block.shape[0]
     tiles = size // 8
     z = [block[8 * b : 8 * b + 8, :] for b in range(tiles)]
@@ -17,8 +17,8 @@
     sub = lax.broadcasted_iota(jnp.int32, (8, size), 0)
     full = lambda v: jnp.broadcast_to(v, (8, size))
     for b in range(tiles):
-        if b == tiles // 2 and middle is not None:
-            middle()
+        if b in hooks:
+            hooks[b]()
         pivots = jnp.ones((8, size), f32)
         for r in range(0, 8, group):
             j = 8 * b + r
@@ -58,12 +58,12 @@
     return jnp.broadcast_to(tile[:, j : j + 1], (8, size))
 
 
-def inverse_factor(z, group=8, size=128, ticks=()):
+def inverse_factor(z, ticks, group=8, size=128):
     n = z.shape[0]
     blocks = n // size
     for k in range(blocks):
         at = slice(k * size, k * size + size)
-        inv = factor_diag(z[at, at], group, ticks[2 * k] if ticks else None)
+        inv = factor_diag(z[at, at], group, {tile: job for (block, tile), job in ticks.items() if block == k})
         z[at, :] = jnp.dot(inv, z[at, :], precision=HI, preferred_element_type=f32)
         z[at, at] = inv
         if k + 1 < blocks:
@@ -73,8 +73,6 @@
             z[below, :] = z[below, :] - lax.dot_general(
                 low, z[at, :], (((0,), (0,)), ((), ())), precision=HI, preferred_element_type=f32
             )
-        if 2 * k + 1 < len(ticks):
-            ticks[2 * k + 1]()
     row = lax.broadcasted_iota(jnp.int32, (n, n), 0) // size
     col = lax.broadcasted_iota(jnp.int32, (n, n), 1) // size
     z[...] = jnp.where(col <= row, z[...], 0.0)
@@ -446,23 +444,27 @@
     axes = (("y", "z"), ("z", "y"))
     across, firsts, fulls, lasts = [], [], [], []
 
-    def turn_sketch():
-        arrive(relay)
-        for i in range(4):
-            for colour in range(2):
-                value = s_buf[colour, place.of(first_axis[colour], steps[i])].reshape(rows, rank).T
-                start = (2 * i + colour) * rows
-                high = value.astype(bf16)
-                st_buf[0, :, start : start + rows] = high
-                st_buf[1, :, start : start + rows] = (value - high.astype(f32)).astype(bf16)
-
-    def multiply(b):
-        block = g_buf[:, :, :, b * deep : b * deep + deep].reshape(8 * rows, deep)
-        out = jnp.dot(st_buf[0], block, preferred_element_type=f32)
-        out += jnp.dot(st_buf[1], block, preferred_element_type=f32)
+    def turn_sketch(i):
+        for colour in range(2):
+            value = s_buf[colour, place.of(first_axis[colour], steps[i])].reshape(rows, rank).T
+            start = (2 * i + colour) * rows
+            high = value.astype(bf16)
+            st_buf[0, :, start : start + rows] = high
+            st_buf[1, :, start : start + rows] = (value - high.astype(f32)).astype(bf16)
+
+    def multiply(b, low, high):
+        block = g_buf[low:high, :, :, b * deep : b * deep + deep].reshape((high - low) * 2 * rows, deep)
+        inner = slice(low * 2 * rows, high * 2 * rows)
+        out = jnp.dot(st_buf[0, :, inner], block, preferred_element_type=f32)
+        out += jnp.dot(st_buf[1, :, inner], block, preferred_element_type=f32)
         for i in range(deep // size):
             p = b * (deep // size) + i
-            x_buf[p // 8, (p // 2) % 4, p % 2] = out[:, i * size : i * size + size].reshape(x_buf.shape[3:])
+            value = out[:, i * size : i * size + size].reshape(x_buf.shape[3:])
+            if high < 4:
+                value += x_buf[p // 8, (p // 2) % 4, p % 2]
+            x_buf[p // 8, (p // 2) % 4, p % 2] = value
+        if low > 0:
+            return
         if b == chunks - 1:
             for p in range(tiles, 32):
                 x_buf[p // 8, (p // 2) % 4, p % 2] = jnp.zeros(x_buf.shape[3:], f32)
@@ -476,29 +478,40 @@
         y_buf[0, i] = total[:, 0]
         y_buf[1, :, i] = total[:, 1]
 
-    def reduce_ring():
+    half_cut = x_buf.shape[-2] // 2
+
+    def reduce_ring(h):
+        at = pl.ds(h * half_cut, half_cut)
         for colour in range(2):
             axis = axes[colour][0]
             far = place.of(axis, 2)
-            firsts.append(links.copy(y_buf.at[colour, far, pl.ds(0, 2)], r_half.at[colour, 0], axis, 1))
-            firsts.append(links.copy(y_buf.at[colour, far, pl.ds(2, 2)], r_half.at[colour, 1], axis, -1))
-
-    def reduce_pass():
+            for side in range(2):
+                src = y_buf.at[colour, far, pl.ds(2 * side, 2), at]
+                firsts.append(links.copy(src, r_half.at[colour, side, :, at], axis, (1, -1)[side]))
+
+    def reduce_pass(h):
+        at = pl.ds(h * half_cut, half_cut)
         for colour in range(2):
             axis = axes[colour][0]
             for side in range(2):
-                firsts[2 * colour + side].wait_recv()
+                firsts[4 * h + 2 * colour + side].wait_recv()
                 to = place.of(axis, (1, -1)[side])
-                y_buf[colour, to, 2 * side : 2 * side + 2] += r_half[colour, side]
-                fulls.append(links.copy(y_buf.at[colour, to], r_full.at[colour, side], axis, (1, -1)[side]))
-
-    def reduce_second():
-        arrive(fulls)
+                y_buf[colour, to, 2 * side : 2 * side + 2, at] += r_half[colour, side, :, at]
+                src = y_buf.at[colour, to, :, at]
+                fulls.append(links.copy(src, r_full.at[colour, side, :, at], axis, (1, -1)[side]))
+
+    def reduce_second(h):
+        at = pl.ds(h * half_cut, half_cut)
+        arrive(fulls[4 * h : 4 * h + 4])
         for colour in range(2):
             axis, other = axes[colour]
-            p_buf[colour] = y_buf[colour, place[axis]] + (r_full[colour, 0] + r_full[colour, 1])
+            p_buf[colour, :, at] = y_buf[colour, place[axis], :, at] + (
+                r_full[colour, 0, :, at] + r_full[colour, 1, :, at]
+            )
             lasts.extend(
-                links.copy(p_buf.at[colour, place.of(other, step)], p_in.at[colour, step - 1], other, step)
+                links.copy(
+                    p_buf.at[colour, place.of(other, step), at], p_in.at[colour, step - 1, at], other, step
+                )
                 for step in (1, 2, 3)
             )
 
@@ -517,46 +530,67 @@
     grams.first()
     mixes.core()
     gather_ring()
+    turn_sketch(3)
+    for b in (0, 1, 2, 3):
+        multiply(b, 3, 4)
     grams.second()
+    mixes.first()
+    for b in (4, 5, 6):
+        multiply(b, 3, 4)
     grams.third()
     gather_relay()
+    turn_sketch(1)
+    turn_sketch(2)
+    multiply(0, 1, 3)
+    multiply(1, 1, 3)
     grams.back2()
+    for b in (2, 3):
+        multiply(b, 1, 3)
+    mixes.second()
+    for b in (4, 5):
+        multiply(b, 1, 3)
     grams.back1()
+    mixes.third()
+    multiply(6, 1, 3)
     lax.fori_loop(1, 32, trade_start, 0)
     mc_buf[:, me] = m_buf[:, :, own_col]
-    turn_sketch()
-    multiply(0)
+    arrive(relay)
+    turn_sketch(0)
+    multiply(0, 0, 1)
+    multiply(1, 0, 1)
     grams.join()
-    mixes.first()
-    multiply(1)
-    multiply(2)
-    multiply(3)
+    mixes.back2()
+    multiply(2, 0, 1)
+    multiply(3, 0, 1)
+    multiply(4, 0, 1)
+    multiply(5, 0, 1)
+    multiply(6, 0, 1)
     grams.end()
-    mixes.second()
-    multiply(4)
-    multiply(5)
-    mixes.third()
-    multiply(6)
 
     for p in range(rank // size):
         z_buf[:, p * size : p * size + size] = totals[0, p // 2, p % 2].reshape(rank, size)
 
     def early():
-        mixes.back2()
         for i in range(SIDE - 1):
             reduce_core(i)
+        mixes.back1()
 
     def start():
-        mixes.back1()
         reduce_core(SIDE - 1)
-        reduce_ring()
-
-    def nothing():
-        pass
+        reduce_ring(0)
+        reduce_ring(1)
 
     inverse_factor(
         z_buf,
-        ticks=(early, start, nothing, mixes.join, reduce_pass, mixes.end, nothing, nothing),
+        ticks={
+            (0, 8): early,
+            (0, 12): start,
+            (1, 4): mixes.join,
+            (1, 12): lambda: reduce_pass(0),
+            (2, 4): lambda: reduce_pass(1),
+            (2, 12): mixes.end,
+            (3, 8): lambda: reduce_second(0),
+        },
     )
 
     def give(step, value, into, sems):
@@ -594,7 +628,7 @@
         corr_buf[start_row:end_row] = jnp.dot(
             z_buf[start_row:end_row, 0:end_row], mixed[0:end_row], precision=HI, preferred_element_type=f32
         )
-    reduce_second()
+    reduce_second(1)
     lax.fori_loop(1, 32, trade_end, 0)
     corr = corr_buf[...]
     shape = turned.shape[1:]
@@ -626,7 +660,7 @@
     cut = rank // 2
     buf = lambda *shape: pltpu.VMEM(shape, f32)
     dma = lambda *shape: pltpu.SemaphoreType.DMA(shape)
-    copies = 32 + 2 * 40 + 40
+    copies = 32 + 2 * 40 + 48
     return pl.pallas_call(
         functools.partial(kernel, tiles),
         out_shape=tuple(jax.ShapeDtypeStruct((n, own_rank, cols), f32) for n in (1, 2)),

time: 119 us -> 112 us (0.941)
  Pallas kernels: 117 us -> 110 us
    pallas_call x1, Pallas kernels: 115 us -> 108 us  [call(): pl.pallas_call(functools.partial(kernel, tiles), out_shape=tuple((jax.Sha...]
where the time goes in v5:
time: 112 us; the launch traced here: 111 us
  Pallas kernels  110 us (98%)
    pallas_call x1, Pallas kernels, call(): pl.pallas_call(functools.partial(kernel, tiles), out_shape=tuple((jax.Sha...  108 us

profile of v5, /device:TPU:0, one launch (start us, length us, event | category | flops | bytes accessed | tf_op | source)
XLA Modules:
  0.0 110.8 jit_solution(2337853967553366493)
XLA Ops:
  0.6 108.2 %shard_map.76 = (f32[1,16,3584]{2,1,0:T(8,128)}, f32[2,16,3584]{2,1,0:T(8,128)}) custom-call(bf16[2,4,128,3584]{3,2,1,0:T(8,128)(2,1)} %bitcast.3, s32[7,512,512]{2,1,0:T(8,128)} %bitcast.4, f32[2,4,4,32,512]{4,3,2,1,0:T(8,128)} %bitcast.5, f32[16,3584]{1,0:T(8,128)} %m1_ref.1, f32[16,3584]{1,0:T(8,128)} %m2_ref.1), custom_call_target="tpu_custom_call" | custom-call | tf_op jit(solution)/shard_map/pallas_call | solution.py:664
  108.8 2.0 %shard_map.77 = (f32[16,3584]{1,0:T(8,128)}, f32[16,3584]{1,0:T(8,128)}, f32[16,3584]{1,0:T(8,128)}) custom-call(f32[1,16,3584]{2,1,0:T(8,128)} %get-tuple-element.5.made_ref, f32[2,16,3584]{2,1,0:T(8,128)} %get-tuple-element.6.turned_ref), custom_call_target="tpu_custom_call" | custom-call | tf_op jit(solution)/shard_map/pallas_call | solution.py:736
